TPU v7x, 32 devices: a whole 2x2x4 slice. The times are simulated.
32 devices in a mesh: dp: 4 (over y, x), fsdp: 8 (over z, core).
Axes of the slice: x: 2, y: 2, z: 4, core: 2. Of those that a mesh axis runs over, the one named last changes fastest.
Arguments:
- tokens: bfloat16 [32768, 768], P(('dp', 'fsdp')), may hold values from -6 to 6
- cotangent: bfloat16 [32768, 768], P(('dp', 'fsdp')), may hold values from -6 to 6
- doc_lengths: int32 [64, 8], P(('dp', 'fsdp')), may hold values from 1 to 160, 512 in all within a row
- w_query: bfloat16 [768, 768], P('fsdp'), may hold values from -0.21875 to 0.21875
- w_key: bfloat16 [768, 768], P('fsdp'), may hold values from -0.21875 to 0.21875
- w_value: bfloat16 [768, 768], P('fsdp'), may hold values from -0.21875 to 0.21875
- w_out: bfloat16 [768, 768], P('fsdp'), may hold values from -0.625 to 0.625
- w_up: bfloat16 [768, 3072], P('fsdp'), may hold values from -0.21875 to 0.21875
- w_down: bfloat16 [3072, 768], P('fsdp'), may hold values from -0.109375 to 0.109375
- pre_gain: bfloat16 [768], P('fsdp'), may hold values from 0.25 to 1.75
- pre_shift: bfloat16 [768], P('fsdp'), may hold values from -1.5 to 1.5
- bias_query: bfloat16 [768], P('fsdp'), may hold values from -2.5 to 2.5
- bias_value: bfloat16 [768], P('fsdp'), may hold values from -2.5 to 2.5
- bias_out: bfloat16 [768], P('fsdp'), may hold values from -2.5 to 2.5
- mid_gain: bfloat16 [768], P('fsdp'), may hold values from 0.25 to 1.75
- mid_shift: bfloat16 [768], P('fsdp'), may hold values from -1.5 to 1.5
- bias_up: bfloat16 [3072], P('fsdp'), may hold values from -2.5 to 2.5
- bias_down: bfloat16 [768], P('fsdp'), may hold values from -1.5 to 1.5
Outputs:
- layer_out: bfloat16 [32768, 768], P(('dp', 'fsdp'))
- input_grad: bfloat16 [32768, 768], P(('dp', 'fsdp'))
- w_query_grad: float32 [768, 768], P('fsdp')
- w_key_grad: float32 [768, 768], P('fsdp')
- w_value_grad: float32 [768, 768], P('fsdp')
- w_out_grad: float32 [768, 768], P('fsdp')
- w_up_grad: float32 [768, 3072], P('fsdp')
- w_down_grad: float32 [3072, 768], P('fsdp')
- pre_gain_grad: float32 [768], P('fsdp')
- pre_shift_grad: float32 [768], P('fsdp')
- bias_query_grad: float32 [768], P('fsdp')
- bias_value_grad: float32 [768], P('fsdp')
- bias_out_grad: float32 [768], P('fsdp')
- mid_gain_grad: float32 [768], P('fsdp')
- mid_shift_grad: float32 [768], P('fsdp')
- bias_up_grad: float32 [3072], P('fsdp')
- bias_down_grad: float32 [768], P('fsdp')
Inputs may be any that keep to these rules, and one draw needn't show every extreme that they name: `doc_lengths`: each row sums to 512; the largest entry of every row is exactly 160.
All inputs are finite; a program needn't handle non-finite values.
Results may differ from a plain program's by a relative error of at most 0.015.
Values may be sent and summed in bfloat16 or wider, within the bound.
No kernel may reach another device: no remote copies, remote signals or barrier semaphores. Data moves between devices by JAX's collectives and lax.ppermute only.
A program may use at most 256 MiB of HBM per device.

v0:
```python
from functools import partial

import jax
import jax.numpy as jnp
from jax import lax
from jax.experimental import pallas as pl
from jax.experimental.pallas import tpu as pltpu
from jax.sharding import PartitionSpec as P

H = 12
HD = 64
SEQ = 512
MOST = 160
BQ = 256
BAND = 416
GAIN_ONE, SHIFT_ONE, QUERY, KEY, VALUE, OUT, GAIN_TWO, SHIFT_TWO, DOWN, UP = range(10)
epsilon = 1e-05
bf16 = jnp.bfloat16
f32 = jnp.float32


def nn(a, b):
    return jnp.dot(a, b, preferred_element_type=f32)


def nt(a, b):
    return lax.dot_general(a, b, (((1,), (1,)), ((), ())), preferred_element_type=f32)


def tn(a, b):
    return lax.dot_general(a, b, (((0,), (0,)), ((), ())), preferred_element_type=f32)


def params(n, mb=56):
    return pltpu.CompilerParams(
        dimension_semantics=("arbitrary",) * n, vmem_limit_bytes=mb * 1024 * 1024
    )


def cost(flops, nbytes, trans=0):
    return pl.CostEstimate(
        flops=int(flops * 50), bytes_accessed=int(nbytes * 50), transcendentals=int(trans)
    )


def moments(v):
    mean = jnp.mean(v, axis=-1, keepdims=True)
    c = v - mean
    inv = lax.rsqrt(jnp.mean(c * c, axis=-1, keepdims=True) + epsilon)
    return c * inv, inv


def shares(place, sides):
    d, z, c = place[0], place[1], place[2]
    for p, (along, near, far) in enumerate(sides):
        core = c ^ p
        parts = ((d, along), (d ^ (1 + core), near), (d ^ (2 - core), far.at[0]), (d ^ 3, far.at[1]))
        for member, view in parts:
            for k in range(3):
                yield member, 2 * (z ^ (k + 1)) + core, view.at[k]


def by_sides(refs):
    return (refs[0], refs[4]), (refs[1:4], refs[5:8])


def start_all(pairs, sem):
    copies = [pltpu.make_async_copy(a, b, sem) for a, b in pairs]
    for copy in copies:
        copy.start()
    return copies


def wait_all(copies):
    for copy in copies:
        copy.wait()


def block_copies(place, refs, out, lead):
    rows = out.shape[1] // 8
    owns, sides = by_sides(refs)
    pairs = []
    for p, own in enumerate(owns):
        s = 2 * place[1] + (place[2] ^ p)
        pairs += [(own.at[4 * lead + b], out.at[b, pl.ds(s * rows, rows), :]) for b in range(4)]
    for member, s, view in shares(place, sides):
        pairs.append((view.at[pl.ds(0, rows), :], out.at[member, pl.ds(s * rows, rows), :]))
    return pairs


def row_copies(place, refs, out, source, skip):
    rows = out.shape[1] // 8
    few = rows // 4
    owns, sides = by_sides(refs)
    pairs = []
    for p, own in enumerate(owns):
        s = 2 * place[1] + (place[2] ^ p)
        for b in range(out.shape[0]):
            pairs.append((own.at[source + b], out.at[b, pl.ds(s * rows, rows), :]))
    for member, s, view in shares(place, sides):
        for b in range(out.shape[0]):
            to = pl.multiple_of(s * rows + member * few, 8)
            pairs.append((view.at[pl.ds(skip + b * few, few), :], out.at[b, pl.ds(to, few), :]))
    return pairs


def split_blocks(place, full, keep, send, b):
    rows = full.shape[0] // 8
    for k in range(4):
        keep[b, k] = full[pl.ds((2 * k + place[2]) * rows, rows), :].astype(bf16)
        send[b, k] = full[pl.ds((2 * k + 1 - place[2]) * rows, rows), :].astype(bf16)


ANY = pl.BlockSpec(memory_space=pl.ANY)


def qkv_kernel(x_ref, w_ref, b_ref, o_ref):
    b = b_ref[0]
    for r in range(x_ref.shape[0] // 256):
        rows = pl.ds(r * 256, 256)
        o_ref[0, rows, :] = (nn(x_ref[rows, :], w_ref[0]) + b).astype(bf16)


def qkv_call(first, w, table):
    rows, d = first.shape
    return pl.pallas_call(
        qkv_kernel,
        grid=(3,),
        in_specs=[
            pl.BlockSpec((rows, d), lambda i: (0, 0)),
            pl.BlockSpec((1, d, d), lambda i: (i, 0, 0)),
            pl.BlockSpec((1, 1, d), lambda i: (QUERY + i, 0, 0)),
        ],
        out_specs=pl.BlockSpec((1, rows, d), lambda i: (i, 0, 0)),
        out_shape=jax.ShapeDtypeStruct((3, rows, d), bf16),
        compiler_params=params(1),
        cost_estimate=cost(6 * rows * d * d, 2 * (rows * d * 4 + 3 * d * d)),
        name="qkv",
    )(first, w, table)


def qkv_fast_kernel(place, x_ref, b_ref, *refs):
    pieces, (o_ref, w_ref, sem) = refs[:8], refs[8:]
    i = pl.program_id(0)

    @pl.when(i == 0)
    def _():
        wait_all(start_all(row_copies(place, pieces, w_ref, 0, 0), sem))

    b = b_ref[0]
    for r in range(x_ref.shape[0] // 256):
        rows = pl.ds(r * 256, 256)
        o_ref[0, rows, :] = (nn(x_ref[rows, :], w_ref[i]) + b).astype(bf16)


def qkv_fast_call(place, first, table, pieces):
    rows, d = first.shape
    return pl.pallas_call(
        qkv_fast_kernel,
        grid_spec=pltpu.PrefetchScalarGridSpec(
            num_scalar_prefetch=1,
            grid=(3,),
            in_specs=[
                pl.BlockSpec((rows, d), lambda i, place: (0, 0)),
                pl.BlockSpec((1, 1, d), lambda i, place: (QUERY + i, 0, 0)),
            ]
            + [ANY] * 8,
            out_specs=[
                pl.BlockSpec((1, rows, d), lambda i, place: (i, 0, 0)),
                pl.BlockSpec((3, d, d), lambda i, place: (0, 0, 0)),
            ],
            scratch_shapes=[pltpu.SemaphoreType.DMA],
        ),
        out_shape=[
            jax.ShapeDtypeStruct((3, rows, d), bf16),
            jax.ShapeDtypeStruct((3, d, d), bf16),
        ],
        compiler_params=params(1),
        cost_estimate=cost(6 * rows * d * d, 2 * (rows * d * 4 + 8 * d * d)),
        name="qkv",
    )(place, first, table, *pieces)


def spans(b):
    return b * BQ, b * (SEQ - BAND)


def attn_fwd_kernel(q_ref, k_ref, v_ref, dr_ref, dc_ref, o_ref, p_ref, bias):
    @pl.when(pl.program_id(1) == 0)
    def _():
        for b in range(2):
            q0, k0 = spans(b)
            same = dc_ref[0, k0 : k0 + BAND, :] == dr_ref[0, :, q0 : q0 + BQ]
            bias[b] = jnp.where(same, 0.0, -3e38)

    low = lax.broadcasted_iota(jnp.int32, (1, 128), 1) < HD
    for b in range(2):
        q0, k0 = spans(b)
        qb = q_ref[0, q0 : q0 + BQ, :] * bf16(HD**-0.5)
        kb = k_ref[0, k0 : k0 + BAND, :]
        vb = v_ref[0, k0 : k0 + BAND, :]
        acc = None
        for hh in range(2):
            mine = low if hh == 0 else jnp.logical_not(low)
            s = nt(kb, jnp.where(mine, qb, bf16(0))) + bias[b]
            e = jnp.exp(s - jnp.max(s, axis=0, keepdims=True))
            p = (e * (1.0 / jnp.sum(e, axis=0, keepdims=True))).astype(bf16)
            p_ref[hh, b] = p
            part = tn(jnp.where(mine, vb, bf16(0)), p)
            acc = part if acc is None else acc + part
        o_ref[q0 : q0 + BQ, :] = acc.T.astype(bf16)


def attn_fwd_call(qkv, doc):
    rows = qkv.shape[1]
    d = qkv.shape[2]
    seqs = rows // SEQ
    hp = d // 128

    def part(i):
        return pl.BlockSpec((1, SEQ, 128), lambda s, h: (i, s, h))

    return pl.pallas_call(
        attn_fwd_kernel,
        grid=(seqs, hp),
        in_specs=[
            part(0),
            part(1),
            part(2),
            pl.BlockSpec((1, 1, SEQ), lambda s, h: (s, 0, 0)),
            pl.BlockSpec((1, SEQ, 1), lambda s, h: (s, 0, 0)),
        ],
        out_specs=[
            pl.BlockSpec((SEQ, 128), lambda s, h: (s, h)),
            pl.BlockSpec((2, 2, BAND, BQ), lambda s, h: (s * hp + h, 0, 0, 0)),
        ],
        out_shape=[
            jax.ShapeDtypeStruct((rows, d), bf16),
            jax.ShapeDtypeStruct((seqs * H, 2, BAND, BQ), bf16),
        ],
        scratch_shapes=[pltpu.VMEM((2, BAND, BQ), f32)],
        compiler_params=params(2),
        cost_estimate=cost(
            seqs * H * 2 * BAND * BQ * 2 * 256, 2 * 4 * rows * d + 4 * seqs * H * BAND * BQ
        ),
        name="attend",
    )(qkv, qkv, qkv, doc[:, None, :], doc[:, :, None])


def attn_bwd_kernel(q_ref, k_ref, v_ref, do_ref, p_ref, o_ref):
    low = lax.broadcasted_iota(jnp.int32, (1, 128), 1) < HD
    scale = bf16(HD**-0.5)
    over = SEQ - BAND
    tails = []
    for b in range(2):
        q0, k0 = spans(b)
        qb = q_ref[0, q0 : q0 + BQ, :] * scale
        dob = do_ref[q0 : q0 + BQ, :]
        kb = k_ref[0, k0 : k0 + BAND, :] * scale
        vb = v_ref[0, k0 : k0 + BAND, :]
        dq = dk = dv = None
        for hh in range(2):
            mine = low if hh == 0 else jnp.logical_not(low)
            p = p_ref[hh, b]
            dom = jnp.where(mine, dob, bf16(0))
            dp = nt(vb, dom)
            pf = p.astype(f32)
            inner = jnp.sum(pf * dp, axis=0, keepdims=True)
            ds = (pf * (dp - inner)).astype(bf16)
            a = nn(p, dom)
            c = nn(ds, jnp.where(mine, qb, bf16(0)))
            g = tn(jnp.where(mine, kb, bf16(0)), ds)
            dv = a if dv is None else dv + a
            dk = c if dk is None else dk + c
            dq = g if dq is None else dq + g
        o_ref[0, q0 : q0 + BQ, :] = dq.T.astype(bf16)
        tails.append((dk, dv))
    for i, (first_part, second_part) in enumerate(zip(*tails)):
        o_ref[i + 1, :over, :] = first_part[:over].astype(bf16)
        o_ref[i + 1, over:BAND, :] = (first_part[over:] + second_part[: BAND - over]).astype(bf16)
        o_ref[i + 1, BAND:, :] = second_part[BAND - over :].astype(bf16)


def attn_bwd_call(qkv, dattn, probs):
    rows = qkv.shape[1]
    d = qkv.shape[2]
    seqs = rows // SEQ
    hp = d // 128

    def part(i):
        return pl.BlockSpec((1, SEQ, 128), lambda s, h: (i, s, h))

    return pl.pallas_call(
        attn_bwd_kernel,
        grid=(seqs, hp),
        in_specs=[
            part(0),
            part(1),
            part(2),
            pl.BlockSpec((SEQ, 128), lambda s, h: (s, h)),
            pl.BlockSpec((2, 2, BAND, BQ), lambda s, h: (s * hp + h, 0, 0, 0)),
        ],
        out_specs=pl.BlockSpec((3, SEQ, 128), lambda s, h: (0, s, h)),
        out_shape=jax.ShapeDtypeStruct((3, rows, d), bf16),
        compiler_params=params(2),
        cost_estimate=cost(
            seqs * H * 2 * BAND * BQ * 2 * 256 * 2, 2 * 7 * rows * d + 4 * seqs * H * BAND * BQ
        ),
        name="attend_back",
    )(qkv, qkv, qkv, dattn, probs)


def row_of(i):
    return pl.BlockSpec((1, 1, 768), lambda *_: (i, 0, 0))


def out_step(a_ref, w, t_ref, bo_ref, g_ref, s_ref, mid_ref, sec_ref):
    mid = t_ref[...].astype(f32) + nn(a_ref[...], w) + bo_ref[0]
    mid_ref[...] = mid
    sc, _ = moments(mid)
    sec_ref[...] = (sc * g_ref[0] + s_ref[0]).astype(bf16)


def out_kernel(a_ref, w_ref, t_ref, bo_ref, g_ref, s_ref, mid_ref, sec_ref):
    out_step(a_ref, w_ref[0], t_ref, bo_ref, g_ref, s_ref, mid_ref, sec_ref)


def out_fast_kernel(place, a_ref, t_ref, bo_ref, g_ref, s_ref, *refs):
    pieces, (mid_ref, sec_ref, w_ref, sem) = refs[:8], refs[8:]

    @pl.when(pl.program_id(0) == 0)
    def _():
        wait_all(start_all(row_copies(place, pieces, w_ref, 8, w_ref.shape[1] // 8), sem))

    out_step(a_ref, w_ref[0], t_ref, bo_ref, g_ref, s_ref, mid_ref, sec_ref)


def out_fast_call(place, attended, tokens, table, pieces):
    rows, d = tokens.shape
    blk = pl.BlockSpec((256, d), lambda i, place: (i, 0))
    return pl.pallas_call(
        out_fast_kernel,
        grid_spec=pltpu.PrefetchScalarGridSpec(
            num_scalar_prefetch=1,
            grid=(rows // 256,),
            in_specs=[blk, blk, row_of(OUT), row_of(GAIN_TWO), row_of(SHIFT_TWO)] + [ANY] * 8,
            out_specs=[blk, blk, pl.BlockSpec((1, d, d), lambda i, place: (0, 0, 0))],
            scratch_shapes=[pltpu.SemaphoreType.DMA],
        ),
        out_shape=[
            jax.ShapeDtypeStruct((rows, d), f32),
            jax.ShapeDtypeStruct((rows, d), bf16),
            jax.ShapeDtypeStruct((1, d, d), bf16),
        ],
        compiler_params=params(1),
        cost_estimate=cost(2 * rows * d * d, rows * d * 10 + 4 * d * d),
        name="project",
    )(place, attended, tokens, table, table, table, *pieces)


def out_call(attended, wo, tokens, table):
    rows, d = tokens.shape
    blk = pl.BlockSpec((256, d), lambda i: (i, 0))
    return pl.pallas_call(
        out_kernel,
        grid=(rows // 256,),
        in_specs=[
            blk, pl.BlockSpec((1, d, d), lambda i: (3, 0, 0)), blk,
            row_of(OUT), row_of(GAIN_TWO), row_of(SHIFT_TWO),
        ],
        out_specs=[blk, blk],
        out_shape=[
            jax.ShapeDtypeStruct((rows, d), f32),
            jax.ShapeDtypeStruct((rows, d), bf16),
        ],
        compiler_params=params(1),
        cost_estimate=cost(2 * rows * d * d, rows * d * 10 + 2 * d * d),
        name="project",
    )(attended, wo, tokens, table, table, table)


def ffn_step(x_ref, g_ref, wu, wd, b, acc_ref, sg_ref, act, hg):
    rows = x_ref.shape[0]
    chunk = 256
    total = jnp.zeros((1, wu.shape[1]), f32)
    def step(r, total):
        at = pl.ds(pl.multiple_of(r * chunk, chunk), chunk)
        h = nn(x_ref[at, :], wu[...]) + b
        ag = nt(g_ref[at, :], wd[...])
        phi = 0.5 + 0.5 * lax.erf(h * (0.5**0.5))
        a = (h * phi).astype(bf16)
        act[at, :] = a
        dens = jnp.exp(-0.5 * (h * h)) * 0.3989422804014327
        hgv = (ag * (phi + h * dens)).astype(bf16)
        hg[at, :] = hgv
        acc_ref[at, :] += nn(a, wd[...])
        sg_ref[at, :] += nt(hgv, wu[...])
        return total + jnp.sum(hgv.astype(f32), axis=0, keepdims=True)

    return lax.fori_loop(0, rows // chunk, step, total)


def ffn_start(start, acc_in, bd_ref, sg_in, acc_ref, sg_ref):
    if start:
        acc_ref[...] = acc_in[...] + bd_ref[0]
        sg_ref[...] = jnp.zeros_like(sg_ref)
    else:
        acc_ref[...] = acc_in[...]
        sg_ref[...] = sg_in[...]


def ffn_kernel(start, x_ref, g_ref, w_ref, b_ref, acc_in, bd_ref, *refs):
    sg_in = None if start else refs[0]
    gw_ref, gb_ref, acc_ref, sg_ref, act, hg = refs[0 if start else 1 :]

    @pl.when(pl.program_id(0) == 0)
    def _():
        ffn_start(start, acc_in, bd_ref, sg_in, acc_ref, sg_ref)

    gb_ref[0] = ffn_step(x_ref, g_ref, w_ref.at[0], w_ref.at[1], b_ref[0], acc_ref, sg_ref, act, hg)
    gw_ref[0] = tn(x_ref[...], hg[...]).astype(bf16)
    gw_ref[1] = tn(act[...], g_ref[...]).astype(bf16)


def ffn_call(lead, second, dgrad, w, table, acc, sg):
    rows, d = second.shape
    n = w.shape[0] // 2
    start = sg is None
    full = pl.BlockSpec((rows, d), lambda j: (0, 0))
    pair = pl.BlockSpec((2, d, d), lambda j: (j, 0, 0))
    return pl.pallas_call(
        partial(ffn_kernel, start),
        grid=(n,),
        in_specs=[
            full, full, pair, pl.BlockSpec((1, 1, d), lambda j: (UP + lead * n + j, 0, 0)),
            full, row_of(DOWN),
        ]
        + ([] if start else [full]),
        out_specs=[pair, pl.BlockSpec((1, 1, d), lambda j: (j, 0, 0)), full, full],
        out_shape=[
            jax.ShapeDtypeStruct((2 * n, d, d), bf16),
            jax.ShapeDtypeStruct((n, 1, d), f32),
            jax.ShapeDtypeStruct((rows, d), f32),
            jax.ShapeDtypeStruct((rows, d), f32),
        ],
        scratch_shapes=[pltpu.VMEM((rows, d), bf16)] * 2,
        compiler_params=params(1),
        cost_estimate=cost(12 * n * rows * d * d, 20 * rows * d + 8 * n * d * d),
        name="feed",
    )(second, dgrad, w, table, acc, table, *([] if start else [sg]))


def ffn_fast_kernel(start, lead, place, x_ref, g_ref, b_ref, acc_in, bd_ref, *refs):
    sg_in, vec_in = (None, None) if start else refs[:2]
    refs = refs[0 if start else 2 :]
    pieces = refs[:8]
    keep, send, vec_ref, acc_ref, sg_ref, w_ref, act, hg, full, sem = refs[8:]
    j = pl.program_id(0)

    @pl.when(j == 0)
    def _():
        copies = start_all(block_copies(place, pieces, w_ref, lead), sem)
        ffn_start(start, acc_in, bd_ref, sg_in, acc_ref, sg_ref)
        vec_ref[...] = jnp.zeros_like(vec_ref) if start else vec_in[...]
        wait_all(copies)

    wu, wd = w_ref.at[2 * j], w_ref.at[2 * j + 1]
    total = ffn_step(x_ref, g_ref, wu, wd, b_ref[0], acc_ref, sg_ref, act, hg)
    vec_ref[pl.ds(2 * lead + j, 1), :] = total
    full[...] = tn(x_ref[...], hg[...]).astype(bf16)
    split_blocks(place, full, keep, send, 0)
    full[...] = tn(act[...], g_ref[...]).astype(bf16)
    split_blocks(place, full, keep, send, 1)


def ffn_fast_call(lead, place, second, dgrad, table, acc, sg, vec, pieces):
    rows, d = second.shape
    start = sg is None
    m = d // 8
    full = pl.BlockSpec((rows, d), lambda j, place: (0, 0))
    half = pl.BlockSpec((2, 4, m, d), lambda j, place: (j, 0, 0, 0))
    rows_of_table = pl.BlockSpec((8, d), lambda j, place: (0, 0))
    return pl.pallas_call(
        partial(ffn_fast_kernel, start, lead),
        grid_spec=pltpu.PrefetchScalarGridSpec(
            num_scalar_prefetch=1,
            grid=(2,),
            in_specs=[
                full, full, pl.BlockSpec((1, 1, d), lambda j, place: (UP + lead * 2 + j, 0, 0)),
                full, row_of(DOWN),
            ]
            + ([] if start else [full, rows_of_table])
            + [ANY] * 8,
            out_specs=[half, half, rows_of_table, full, full],
            scratch_shapes=[pltpu.VMEM((4, d, d), bf16)]
            + [pltpu.VMEM((rows, d), bf16)] * 2
            + [pltpu.VMEM((d, d), bf16), pltpu.SemaphoreType.DMA],
        ),
        out_shape=[
            jax.ShapeDtypeStruct((4, 4, m, d), bf16),
            jax.ShapeDtypeStruct((4, 4, m, d), bf16),
            jax.ShapeDtypeStruct((8, d), f32),
            jax.ShapeDtypeStruct((rows, d), f32),
            jax.ShapeDtypeStruct((rows, d), f32),
        ],
        compiler_params=params(1),
        cost_estimate=cost(24 * rows * d * d, 20 * rows * d + 16 * d * d),
        name="feed",
    )(place, second, dgrad, table, acc, table, *([] if start else [sg, vec]), *pieces)


def norm_back(grad, sc, inv, gain):
    t = grad * gain
    return inv * (
        t - jnp.mean(t, axis=-1, keepdims=True) - sc * jnp.mean(t * sc, axis=-1, keepdims=True)
    )


def mid_kernel(
    place, sg_ref, mid_ref, dy_ref, a_ref, w_ref, g_ref, acc_ref, vec_in,
    mg_ref, ag_ref, vec_ref, lo_ref, wg_ref, *rest,
):
    i = pl.program_id(0)
    wacc = rest[-1]

    @pl.when(i == 0)
    def _():
        wacc[...] = jnp.zeros_like(wacc)
        vec_ref[...] = vec_in[...]

    lo_ref[...] = acc_ref[...].astype(bf16)
    sc, inv = moments(mid_ref[...])
    sg = sg_ref[...]
    dy = dy_ref[...].astype(f32)
    mg = dy + norm_back(sg, sc, inv, g_ref[0])
    mg_ref[...] = mg
    br = mg.astype(bf16)
    vec_ref[4:5, :] += jnp.sum(sg * sc, axis=0, keepdims=True)
    vec_ref[5:6, :] += jnp.sum(sg, axis=0, keepdims=True)
    vec_ref[6:7, :] += jnp.sum(br.astype(f32), axis=0, keepdims=True)
    vec_ref[7:8, :] += jnp.sum(dy, axis=0, keepdims=True)
    ag_ref[...] = nt(br, w_ref[0]).astype(bf16)
    wacc[...] += tn(a_ref[...], br)

    @pl.when(i == pl.num_programs(0) - 1)
    def _():
        if len(rest) == 1:
            wg_ref[0] = wacc[...].astype(bf16)
        else:
            split_blocks(place, wacc, wg_ref, rest[0], 0)


def mid_call(place, sg, mid, dy, attended, wo, table, acc, vec, split):
    rows, d = sg.shape
    blk = pl.BlockSpec((256, d), lambda i, place: (i, 0))
    grad = (1, 4, d // 8, d) if split else (1, d, d)
    last = wo.shape[0] - 1
    return pl.pallas_call(
        mid_kernel,
        grid_spec=pltpu.PrefetchScalarGridSpec(
            num_scalar_prefetch=1,
            grid=(rows // 256,),
            in_specs=[
                blk, blk, blk, blk, pl.BlockSpec((1, d, d), lambda i, place: (last, 0, 0)),
                row_of(GAIN_TWO), blk, pl.BlockSpec((8, d), lambda i, place: (0, 0)),
            ],
            out_specs=[blk, blk, pl.BlockSpec((8, d), lambda i, place: (0, 0)), blk]
            + [pl.BlockSpec(grad, lambda i, place: (0,) * len(grad))] * (2 if split else 1),
            scratch_shapes=[pltpu.VMEM((d, d), f32)],
        ),
        out_shape=[
            jax.ShapeDtypeStruct((rows, d), f32),
            jax.ShapeDtypeStruct((rows, d), bf16),
            jax.ShapeDtypeStruct((8, d), f32),
            jax.ShapeDtypeStruct((rows, d), bf16),
        ]
        + [jax.ShapeDtypeStruct(grad, bf16)] * (2 if split else 1),
        compiler_params=params(1),
        cost_estimate=cost(4 * rows * d * d, rows * d * 22 + 4 * d * d),
        name="middle_back",
    )(place, sg, mid, dy, attended, wo, table, acc, vec)


def wgrad_kernel(x_ref, g_ref, o_ref, b_ref):
    o_ref[0] = tn(x_ref[...], g_ref[0]).astype(bf16)
    b_ref[0] = jnp.sum(g_ref[0].astype(f32), axis=0, keepdims=True)


def wgrad_call(first, grads):
    rows, d = first.shape
    return pl.pallas_call(
        wgrad_kernel,
        grid=(3,),
        in_specs=[
            pl.BlockSpec((rows, d), lambda i: (0, 0)),
            pl.BlockSpec((1, rows, d), lambda i: (i, 0, 0)),
        ],
        out_specs=[
            pl.BlockSpec((1, d, d), lambda i: (i, 0, 0)),
            pl.BlockSpec((1, 1, d), lambda i: (i, 0, 0)),
        ],
        out_shape=[
            jax.ShapeDtypeStruct((3, d, d), bf16),
            jax.ShapeDtypeStruct((3, 1, d), f32),
        ],
        compiler_params=params(1),
        cost_estimate=cost(6 * rows * d * d, 2 * (rows * d * 4 + 3 * d * d)),
        name="weight_back",
    )(first, grads)


def wgrad_fast_kernel(place, x_ref, g_ref, vec_in, keep, send, vec_ref, full):
    i = pl.program_id(0)

    @pl.when(i == 0)
    def _():
        vec_ref[:8, :] = vec_in[...]
        vec_ref[8:, :] = jnp.zeros_like(vec_in)

    full[...] = tn(x_ref[...], g_ref[0])
    vec_ref[pl.ds(8 + i, 1), :] = jnp.sum(g_ref[0].astype(f32), axis=0, keepdims=True)
    split_blocks(place, full, keep, send, 0)


def wgrad_fast_call(place, first, grads, vec):
    rows, d = first.shape
    m = d // 8
    half = pl.BlockSpec((1, 4, m, d), lambda i, place: (i, 0, 0, 0))
    return pl.pallas_call(
        wgrad_fast_kernel,
        grid_spec=pltpu.PrefetchScalarGridSpec(
            num_scalar_prefetch=1,
            grid=(3,),
            in_specs=[
                pl.BlockSpec((rows, d), lambda i, place: (0, 0)),
                pl.BlockSpec((1, rows, d), lambda i, place: (i, 0, 0)),
                pl.BlockSpec((8, d), lambda i, place: (0, 0)),
            ],
            out_specs=[half, half, pl.BlockSpec((16, d), lambda i, place: (0, 0))],
            scratch_shapes=[pltpu.VMEM((d, d), f32)],
        ),
        out_shape=[
            jax.ShapeDtypeStruct((3, 4, m, d), bf16),
            jax.ShapeDtypeStruct((3, 4, m, d), bf16),
            jax.ShapeDtypeStruct((16, d), f32),
        ],
        compiler_params=params(1),
        cost_estimate=cost(6 * rows * d * d, 2 * (rows * d * 4 + 3 * d * d)),
        name="weight_back",
    )(place, first, grads, vec)


def input_kernel(start, g_ref, w_ref, t_ref, mg_ref, gain_ref, *refs):
    o_ref, vec_ref = refs[-2:]

    @pl.when(pl.program_id(0) == 0)
    def _():
        vec_ref[...] = jnp.zeros_like(vec_ref) if start else refs[0][...]

    fg = nt(g_ref[0], w_ref[0]) + nt(g_ref[1], w_ref[1]) + nt(g_ref[2], w_ref[2])
    sc, inv = moments(t_ref[...].astype(f32))
    o_ref[...] = (mg_ref[...] + norm_back(fg, sc, inv, gain_ref[0])).astype(bf16)
    vec_ref[0:1, :] += jnp.sum(fg * sc, axis=0, keepdims=True)
    vec_ref[1:2, :] += jnp.sum(fg, axis=0, keepdims=True)


def input_call(grads, w, tokens, mg, table, skip, steps, before=()):
    rows, d = tokens.shape
    blk = pl.BlockSpec((256, d), lambda i: (skip + i, 0))
    vec = pl.BlockSpec((8, d), lambda i: (0, 0))
    start = not before
    return pl.pallas_call(
        partial(input_kernel, start),
        grid=(steps,),
        in_specs=[
            pl.BlockSpec((3, 256, d), lambda i: (0, skip + i, 0)),
            pl.BlockSpec((3, d, d), lambda i: (0, 0, 0)),
            blk,
            blk,
            row_of(GAIN_ONE),
        ]
        + ([] if start else [vec, ANY]),
        out_specs=[blk, vec],
        out_shape=[
            jax.ShapeDtypeStruct((rows, d), bf16),
            jax.ShapeDtypeStruct((8, d), f32),
        ],
        input_output_aliases={} if start else {6: 0},
        compiler_params=params(1),
        cost_estimate=cost(1536 * steps * d * d, 256 * steps * d * 14 + 6 * d * d),
        name="input_back",
    )(grads, w, tokens, mg, table, *([] if start else [before[1], before[0]]))


CORE = 1
ALONG = (2, 4, 6)
GROUP = (8, 16, 24)


def hop(x, mask):
    return lax.ppermute(x, ("dp", "fsdp"), [(i, i ^ mask) for i in range(32)])


def group_hop(x, second):
    pairs = [(i, i ^ (GROUP[0] if i % 2 == second else GROUP[1])) for i in range(32)]
    return lax.ppermute(x, ("dp", "fsdp"), pairs)


def pick(x, index, axis=0):
    return lax.dynamic_index_in_dim(x, index, axis, keepdims=False)


def after(deps, *xs):
    return lax.optimization_barrier((*xs, *deps))[: len(xs)]


def wide(x):
    return x.astype(f32)


def add_core(keep, got):
    return (wide(keep) + wide(got)).astype(bf16)


def quarter(x, index, axis):
    n = x.shape[axis] // 4
    return lax.dynamic_slice_in_dim(x, index * n, n, axis)


def add_two(a, b):
    return (wide(a) + wide(b)).astype(bf16)


def turn(x, bits):
    for axis, bit in enumerate(bits):
        x = jnp.where(bit == 0, x, jnp.flip(x, axis))
    return x


def add_all(first, others):
    total = wide(first)
    for other in others:
        total = total + wide(other)
    return total.astype(bf16)


def segment_ids(lengths):
    ends = jnp.cumsum(lengths, axis=-1)
    places = jnp.arange(SEQ, dtype=jnp.int32)
    return jnp.sum((places[None, :, None] >= ends[:, None, :]).astype(jnp.int32), axis=-1)


def pack_vectors(pre_gain, pre_shift, bias_query, bias_value, bias_out, mid_gain, mid_shift, bias_up, bias_down):
    none = jnp.zeros_like(bias_query)
    return jnp.concatenate(
        [pre_gain, pre_shift, bias_query, none, bias_value, bias_out, mid_gain, mid_shift, bias_down, bias_up]
    )[None]


def make_table(small):
    shards = small.shape[0]
    n = small.shape[1] * shards // 768
    return small.reshape(shards, n, -1).transpose(1, 0, 2).reshape(n, 1, 768).astype(f32)


def order_hidden(w_up, w_down, shards):
    m, d = w_up.shape[0], w_up.shape[0] * shards
    parts = w_down.shape[0] // m
    up = w_up.reshape(m, shards, parts, m).transpose(2, 0, 1, 3).reshape(parts, m, d)
    return jnp.stack([up, w_down.reshape(parts, m, d)], 1).reshape(2 * parts, m, d)


VEC_ROWS = (0, 1, 16, 18, 10, 8, 9)
DOWN_ROW, UP_ROW = 11, 20


def outputs(layer_out, input_grad, attn, feed, vec, factor, shards):
    m, d = attn[0].shape
    parts = len(feed) // 2
    vec = vec * factor
    up = jnp.stack(feed[0::2]).reshape(parts, m, shards, m).transpose(1, 2, 0, 3)
    return (
        layer_out,
        input_grad,
        *(wide(g) * factor for g in attn),
        wide(up.reshape(m, parts * d)) * factor,
        wide(jnp.concatenate(feed[1::2])) * factor,
        *(vec[i] for i in VEC_ROWS),
        vec[UP_ROW:].reshape(-1),
        vec[DOWN_ROW],
    )


def body_fast(tokens, cotangent, doc_lengths, w_query, w_key, w_value, w_out, w_up, w_down, *vectors):
    rows, d = tokens.shape
    n = d // 8
    dp, at = lax.axis_index("dp"), lax.axis_index("fsdp")
    z, core = at // 2, at % 2
    place = jnp.stack([dp, z, core]).astype(jnp.int32)
    one, two = 1 + core, 2 - core

    quarters = [quarter(w, dp, 0) for w in (w_query, w_key, w_value, w_out)]
    attn_mine = jnp.concatenate(quarters[:3])
    attn_z = [hop(attn_mine, m) for m in ALONG]
    attn_along = jnp.stack(attn_z)
    attn_near = group_hop(attn_along, 0)
    attn_own = jnp.stack([w_query, w_key, w_value])
    attn_own_cross = hop(attn_own, CORE)
    small = pack_vectors(*after([attn_along], *vectors))
    width = small.shape[1]
    low = jnp.pad(small[0], (0, 8 * d - width)).reshape(8, d)
    low = jnp.concatenate([low, hop(low, CORE)])
    attn_far = jnp.stack([attn_along, attn_near])
    (low,) = after([attn_far], low)
    low_across = hop(low, ALONG[1])
    low_beside = hop(jnp.stack([low, low_across]), ALONG[0])
    lows = jnp.stack([low, low_beside[0], low_across, low_beside[1]])
    small = lows.reshape(2, 2, 2, 8 * d)[..., :width]
    table = make_table(turn(small, (z // 2, z % 2, core)).reshape(8, width))
    attn_along_cross = hop(attn_along, CORE)
    attn_far = group_hop(attn_far, 1)
    attn_near_cross = hop(attn_near, CORE)
    attn_far_cross = hop(attn_far, CORE)

    feed_own = order_hidden(w_up, w_down, 8)
    mine_one = jnp.concatenate([pick(feed_own[:4], dp), quarters[3]])
    tokens_late, lengths_late, mine_one = after([attn_along], tokens, doc_lengths, mine_one)
    mine_two = pick(feed_own[4:], dp)
    feed_own = jnp.concatenate([feed_own, w_out[None]])
    across_one = hop(mine_one, ALONG[1])
    mine_late, across_late = after([attn_near], mine_one, across_one)
    beside_one = hop(jnp.stack([mine_late, across_late]), ALONG[0])
    beside_one, mine_two = after([attn_far], beside_one, mine_two)
    along_one = jnp.stack([beside_one[0], across_one, beside_one[1]])
    near_one = group_hop(along_one, 0)
    across_two = hop(mine_two, ALONG[1])

    doc = segment_ids(lengths_late)
    scaled, _ = moments(wide(tokens_late))
    first = (scaled * table[GAIN_ONE] + table[SHIFT_ONE]).astype(bf16)
    qkv, attn_w = qkv_fast_call(
        place, first, table,
        [attn_own, attn_along, attn_near, attn_far]
        + [attn_own_cross, attn_along_cross, attn_near_cross, attn_far_cross],
    )
    feed_own_late, along_one, near_one, mine_two, across_two = after(
        [qkv], feed_own, along_one, near_one, mine_two, across_two
    )
    (qkv,) = after([near_one, across_two], qkv)
    far_one = group_hop(jnp.stack([along_one, near_one]), 1)
    beside_two = hop(jnp.stack([mine_two, across_two]), ALONG[0])
    feed_cross = hop(feed_own_late, CORE)
    pieces_one = [feed_cross, hop(along_one, CORE), hop(near_one, CORE)]
    attended, probs = attn_fwd_call(qkv, doc)
    far_one, beside_two, attended_late = after([attended], far_one, beside_two, attended)
    (attended_late,) = after([far_one, beside_two], attended_late)
    pieces_one = [feed_own, along_one, near_one, far_one, *pieces_one, hop(far_one, CORE)]
    along_two = jnp.stack([beside_two[0], across_two, beside_two[1]])
    near_two = group_hop(along_two, 0)
    middle, second, wo = out_fast_call(place, attended_late, tokens, table, pieces_one)
    along_two, near_two, second = after([middle], along_two, near_two, second)
    (second,) = after([near_two], second)
    far_two = group_hop(jnp.stack([along_two, near_two]), 1)
    pieces_two = [along_two, near_two, far_two]
    pieces_two = [feed_own, *pieces_two, feed_cross, *(hop(x, CORE) for x in pieces_two)]

    def first_hop(parts):
        return group_hop(jnp.stack([parts(dp ^ one), parts(dp ^ 3)]), 0)

    def fold(parts, got):
        return add_two(parts(dp), got[0]), add_two(parts(dp ^ two), got[1])

    def beside(x):
        return jnp.stack([pick(x, z ^ 1), pick(x, z ^ 3)])

    def across(x, got):
        return add_two(pick(x, z), got[0]), add_two(pick(x, z ^ 2), got[1])

    keep_one, send_one, vec, acc, sg = ffn_fast_call(
        0, place, second, cotangent, table, middle, None, None, pieces_one
    )
    (send_one,) = after([far_two], send_one)
    got_one = hop(send_one, CORE)
    parts_one = lambda i: add_two(pick(keep_one, i), pick(got_one, i))
    near_one = first_hop(parts_one)
    (sg,) = after([got_one], sg)
    keep_two, send_two, vec, acc, sg = ffn_fast_call(
        1, place, second, cotangent, table, acc, sg, vec, pieces_two
    )
    got_two = hop(send_two, CORE)
    (sg,) = after([near_one], sg)
    mine_one, far_one = fold(parts_one, near_one)
    (sg,) = after([far_one], sg)
    far_one = group_hop(far_one, 1)
    mid_grad, attended_grad, vec, layer_out, keep_out, send_out = mid_call(
        place, sg, middle, cotangent, attended, wo, table, acc, vec, True
    )
    got_out = hop(send_out, CORE)
    (attended_grad,) = after([far_one, got_two, got_out], attended_grad)
    sum_one = add_two(mine_one, far_one)
    beside_one = hop(beside(sum_one), ALONG[0])

    def parts_two(i):
        out = add_two(quarter(keep_out[0], i, 1), quarter(got_out[0], i, 1))
        return jnp.concatenate([add_two(pick(keep_two, i), pick(got_two, i)), out], 1)

    near_two = first_hop(parts_two)
    grads = attn_bwd_call(qkv, attended_grad, probs)
    (beside_one,) = after([grads], beside_one)
    mine_one, across_one = across(sum_one, beside_one)
    mine_two, far_two = fold(parts_two, near_two)
    (grads,) = after([across_one, far_two], grads)
    across_one = hop(across_one, ALONG[1])
    far_two = group_hop(far_two, 1)
    keep_attn, send_attn, vec = wgrad_fast_call(place, first, grads, vec)
    (send_attn,) = after([across_one, far_two], send_attn)
    got_attn = hop(send_attn, CORE)
    sum_two = add_two(mine_two, far_two)
    beside_two = beside(sum_two)
    (got_attn,) = after([beside_two], got_attn)
    parts_attn = lambda i: add_two(quarter(keep_attn, i, 2), quarter(got_attn, i, 2))
    near_attn = jnp.stack([parts_attn(dp ^ one), parts_attn(dp ^ 3)])
    (grads,) = after([beside_two, near_attn], grads)
    beside_two = hop(beside_two, ALONG[0])
    near_attn = group_hop(near_attn, 0)
    input_grad, in_vec = input_call(grads, attn_w, tokens, mid_grad, table, 0, rows // 256)
    near_attn, beside_two = after([in_vec], near_attn, beside_two)
    mine_attn, far_attn = fold(parts_attn, near_attn)
    mine_two, across_two = across(sum_two, beside_two)
    mine_one, across_one, in_vec, vec = after([far_attn], mine_one, across_one, in_vec, vec)
    far_attn = group_hop(far_attn, 1)
    across_two = hop(across_two, ALONG[1])

    in_vec = in_vec[:2] + hop(in_vec[:2], CORE)
    vec = vec.reshape(16, 4, 2, n).transpose(2, 1, 0, 3)
    vec = pick(vec, core) + hop(pick(vec, 1 - core), CORE)
    vec = vec.reshape(4, 16 * n // d, d).astype(bf16)
    low = jnp.concatenate(
        [vec, jnp.broadcast_to(in_vec.astype(bf16)[None], (4, 2, d)), jnp.zeros((4, 4, d), bf16)], 1
    )
    far_attn, low = after((), far_attn, low)
    attn_sum = add_two(mine_attn, far_attn)
    many = 3 * attn_sum.shape[2]
    rest = attn_sum.transpose(1, 0, 2, 3).reshape(4, many, d)
    rest = jnp.concatenate([rest, low], 1)
    beside_rest = beside(rest)
    (across_two,) = after([beside_rest], across_two)
    beside_rest = hop(beside_rest, ALONG[0])
    final_feed = jnp.concatenate([add_two(mine_one, across_one), add_two(mine_two, across_two)])
    feed_near = group_hop(final_feed, 0)
    mine_rest, across_rest = across(rest, beside_rest)
    final_feed, feed_near = after([across_rest], final_feed, feed_near)
    feed_far = group_hop(jnp.stack([final_feed, feed_near]), 1)
    final_rest = add_two(mine_rest, hop(across_rest, ALONG[1]))
    (final_rest,) = after([feed_far], final_rest)
    final_rest = jnp.stack([final_rest] + [hop(final_rest, m) for m in GROUP])
    vec = jnp.sum(wide(final_rest[:, many : many + 4]), axis=0)
    in_vec = lax.dynamic_slice_in_dim(vec[2:], at * n, n, 1)
    vec = vec[:2].reshape(16, n)
    none = jnp.zeros((6, n), f32)
    vec = jnp.concatenate([in_vec, none, vec[4:8], none[:4], vec[8:12], vec[:4]])
    final_feed = jnp.stack([final_feed, feed_near, feed_far[0], feed_far[1]])
    order = lambda b: jnp.where(b == one, 1, jnp.where(b == two, 2, b))
    final_attn = [pick(final_rest, dp ^ b)[:many].reshape(3, many // 3, d) for b in range(4)]
    final_feed = [pick(final_feed, order(dp ^ b)) for b in range(4)]
    attn = [jnp.concatenate([x[i] for x in final_attn]) for i in range(3)]
    attn.append(jnp.concatenate([x[2 * n :] for x in final_feed]))
    feed = [x[:n] for x in final_feed] + [x[n : 2 * n] for x in final_feed]
    factor = (32 * rows) ** (-0.5)
    return outputs(layer_out, input_grad, attn, feed, vec, factor, 8)


def gather(local):
    return lax.all_gather(local, "fsdp", axis=1, tiled=True)


def reduce(grad):
    part = lax.psum_scatter(wide(grad), "fsdp", scatter_dimension=1, tiled=True)
    total = lax.psum(part.astype(bf16), "dp")
    return [total[b] for b in range(grad.shape[0])]


def body_plain(tokens, cotangent, doc_lengths, w_query, w_key, w_value, w_out, w_up, w_down, *vectors):
    rows = tokens.shape[0]
    shards, groups = lax.axis_size("fsdp"), lax.axis_size("dp")
    table = make_table(lax.all_gather(pack_vectors(*vectors), "fsdp", axis=0, tiled=True))
    attn_w = gather(jnp.stack([w_query, w_key, w_value, w_out]))
    feed_own = order_hidden(w_up, w_down, shards)
    doc = segment_ids(doc_lengths)
    scaled, _ = moments(wide(tokens))
    first = (scaled * table[GAIN_ONE] + table[SHIFT_ONE]).astype(bf16)
    qkv = qkv_call(first, attn_w, table)
    attended, probs = attn_fwd_call(qkv, doc)
    middle, second = out_call(attended, attn_w, tokens, table)
    acc, sg = middle, None
    feed = []
    up_bias = []
    for lead in range(feed_own.shape[0] // 4):
        w = gather(feed_own[4 * lead : 4 * lead + 4])
        grad, bias_grad, acc, sg = ffn_call(lead, second, cotangent, w, table, acc, sg)
        feed += reduce(grad)
        up_bias.append(bias_grad)
    mid_grad, attended_grad, mid_vec, layer_out, out_grad = mid_call(
        jnp.zeros((3,), jnp.int32), sg, middle, cotangent, attended, attn_w, table, acc,
        jnp.zeros((8, tokens.shape[1]), f32), False,
    )
    grads = attn_bwd_call(qkv, attended_grad, probs)
    proj_grad, proj_bias = wgrad_call(first, grads)
    input_grad, in_vec = input_call(grads, attn_w, tokens, mid_grad, table, 0, tokens.shape[0] // 256)
    attn = reduce(jnp.concatenate([proj_grad, out_grad]))
    none = jnp.zeros((1,) + proj_bias.shape[2:], f32)
    mid_vec = jnp.roll(mid_vec, 4, 0)
    vec = jnp.concatenate([in_vec, mid_vec, proj_bias[:, 0], none] + [x[:, 0] for x in up_bias])
    vec = vec.reshape(vec.shape[0], shards, -1).transpose(1, 0, 2)
    vec = lax.psum(lax.psum_scatter(vec, "fsdp", scatter_dimension=0, tiled=True), "dp")[0]
    factor = (groups * shards * rows) ** (-0.5)
    return outputs(layer_out, input_grad, attn, feed, vec, factor, shards)


def solution(mesh):
    both = P(("dp", "fsdp"), None)
    matrix, vector = P("fsdp", None), P("fsdp")
    fast = mesh.shape["dp"] == 4 and mesh.shape["fsdp"] == 8
    return jax.shard_map(
        body_fast if fast else body_plain,
        mesh=mesh,
        in_specs=(both,) * 3 + (matrix,) * 6 + (vector,) * 9,
        out_specs=(both,) * 2 + (matrix,) * 6 + (vector,) * 9,
        check_vma=False,
    )
```

profile of v0, /device:TPU:0, one launch (start us, length us, event | category | flops | bytes accessed | tf_op | source)
XLA Modules:
  0.0 293.3 jit_solution(9620288667299715855)
XLA Ops:
  2.3 3.1 %collective-permute-start = (bf16[72,768]{1,0:T(8,128)(2,1)S(1)}, bf16[72,768]{1,0:T(8,128)(2,1)S(1)}, u32[]{:S(2)}, u32[]{:S(2)}) collective-permute-start(bf16[72,768]{1,0:T(8,128)(2,1)S(1)} %pad_maximum_fusion.22), channel_id=1, source_target_pairs={{0,2},{1,3},{2,0},{3,1},{4,6},{5,7},{6,4},{7,5},{8,10},{9,11},{10,... | collective-permute-start | bytes 331784 | tf_op jit(solution)/shard_map/ppermute | solution.py:701
  5.4 2.6 collective-permute-start.1
  8.0 1.9 pad_maximum_fusion.12.refs_0_
  17.1 1.7 fusion.39
  18.9 1.7 collective-permute-start.4
  22.3 2.4 collective-permute-start.3
  26.3 2.6 collective-permute-start.10
  30.6 1.5 collective-permute-start.6
  32.1 2.7 collective-permute-done.3
  35.3 1.9 collective-permute-start.5
  37.2 2.5 collective-permute-done.11
  41.4 1.8 fusion.5.x_ref
  43.9 2.2 collective-permute-done.5
  47.0 1.6 collective-permute-start.7
  48.6 2.4 collective-permute-start.8
  51.9 9.7 %qkv.1 = (bf16[3,1024,768]{2,1,0:T(8,128)(2,1)}, bf16[3,768,768]{2,1,0:T(8,128)(2,1)}) custom-call(s32[3]{0:T(128)} %pad_add_fusion.place, bf16[1024,768]{1,0:T(8,128)(2,1)} %fusion.5.x_ref, f32[13,1,768]{2,1,0:T(1,128)} %convert_element_type.471.b_ref.bo_ref.g_ref.s_ref.bd_ref.gain_ref, bf16[3,96,768]{2,1,0:T(8,128)(2,1)} %pad_maximum_fusion.12.refs_0_, ...), custom_call_target="tpu_custom_call" | custom-call | flops 181193932800 | bytes 786432000 | tf_op jit(solution)/shard_map/qkv/pallas_call | solution.py:158
  66.3 16.9 %attend.1 = (bf16[1024,768]{1,0:T(8,128)(2,1)}, bf16[24,2,416,256]{3,2,1,0:T(8,128)(2,1)}) custom-call(bf16[3,1024,768]{2,1,0:T(8,128)(2,1)} %get-tuple-element.119.q_ref.k_ref.v_ref, bf16[3,1024,768]{2,1,0:T(8,128)(2,1)} %get-tuple-element.119.q_ref.k_ref.v_ref, bf16[3,1024,768]{2,1,0:T(8,128)(2,1)} %get-tuple-element.119.q_ref.k_ref.v_ref, ...), custom_call_target="tpu_custom_call" | custom-call | flops 130862284800 | bytes 825753600 | tf_op jit(solution)/shard_map/attend/pallas_call | solution.py:223
  85.2 1.5 collective-permute-start.18
  89.9 7.3 %project.1 = (f32[1024,768]{1,0:T(8,128)}, bf16[1024,768]{1,0:T(8,128)(2,1)}, bf16[1,768,768]{2,1,0:T(8,128)(2,1)}) custom-call(s32[3]{0:T(128)} %pad_add_fusion.place, bf16[1024,768]{1,0:T(8,128)(2,1)} %get-tuple-element.125.a_ref, bf16[1024,768]{1,0:T(8,128)(2,1)} %t_ref.3, f32[13,1,768]{2,1,0:T(1,128)} %convert_element_type.471.b_ref.bo_ref.g_ref.s_ref.bd_ref.gain_ref, ...), custom_call_target="tpu_custom_call" | custom-call | flops 60397977600 | bytes 511180800 | tf_op jit(solution)/shard_map/project/pallas_call | solution.py:341
  99.4 25.9 %feed.2 = (bf16[4,4,96,768]{3,2,1,0:T(8,128)(2,1)}, bf16[4,4,96,768]{3,2,1,0:T(8,128)(2,1)}, f32[8,768]{1,0:T(8,128)}, f32[1024,768]{1,0:T(8,128)}, f32[1024,768]{1,0:T(8,128)}) custom-call(s32[3]{0:T(128)} %pad_add_fusion.place, bf16[1024,768]{1,0:T(8,128)(2,1)} %get-tuple-element.131.x_ref, bf16[1024,768]{1,0:T(8,128)(2,1)} %dy_ref.1, ...), custom_call_target="tpu_custom_call" | custom-call | flops 724775731200 | bytes 1258291200 | tf_op jit(solution)/shard_map/feed/pallas_call | solution.py:483
  126.4 3.8 %collective-permute-done.24 = bf16[4,4,96,768]{3,2,1,0:T(8,128)(2,1)S(1)} collective-permute-done((bf16[4,4,96,768]{3,2,1,0:T(8,128)(2,1)}, bf16[4,4,96,768]{3,2,1,0:T(8,128)(2,1)S(1)}, u32[]{:S(2)}, u32[]{:S(2)}) %collective-permute-start.24) | collective-permute-done | bytes 2359328 | tf_op jit(solution)/shard_map/ppermute | solution.py:701
  130.2 2.4 add_convert_fusion.10
  135.3 27.3 %feed.3 = (bf16[4,4,96,768]{3,2,1,0:T(8,128)(2,1)}, bf16[4,4,96,768]{3,2,1,0:T(8,128)(2,1)}, f32[8,768]{1,0:T(8,128)}, f32[1024,768]{1,0:T(8,128)}, f32[1024,768]{1,0:T(8,128)}) custom-call(s32[3]{0:T(128)} %pad_add_fusion.place, bf16[1024,768]{1,0:T(8,128)(2,1)} %get-tuple-element.131.x_ref, bf16[1024,768]{1,0:T(8,128)(2,1)} %dy_ref.1, ...), custom_call_target="tpu_custom_call" | custom-call | flops 724775731200 | bytes 1258291200 | tf_op jit(solution)/shard_map/feed/pallas_call | solution.py:483
  164.2 1.6 collective-permute-start.29
  165.7 11.9 %middle_back.1 = (f32[1024,768]{1,0:T(8,128)}, bf16[1024,768]{1,0:T(8,128)(2,1)}, f32[8,768]{1,0:T(8,128)}, bf16[1024,768]{1,0:T(8,128)(2,1)}, bf16[1,4,96,768]{...) custom-call(s32[3]{0:T(128)} %pad_add_fusion.place, f32[1024,768]{1,0:T(8,128)} %get-tuple-element.142.sg_ref, ...), custom_call_target="tpu_custom_call" | custom-call | flops 120795955200 | bytes 983040000 | tf_op jit(solution)/shard_map/middle_back/pallas_call | solution.py:558
  177.8 1.8 fusion.8
  182.0 3.3 %fusion.14 = (bf16[4,96,768]{2,1,0:T(8,128)(2,1)}, bf16[4,96,768]{2,1,0:T(8,128)(2,1)S(1)}, bf16[4,96,768]{2,1,0:T(8,128)(2,1)S(1)}, bf16[4,96,768]{2,1,0:T(8,128)(2,1)}) fusion(bf16[4,4,96,768]{3,2,1,0:T(8,128)(2,1)} %collective-permute-done.30, s32[]{:T(128)S(6)} %select_n.174, bf16[4,4,96,768]{3,2,1,0:T(8,128)(2,1)S(1)} %copy-done.5, s32[]{:T(128)S(6)} %select_n.185, ...), kind=kLoop, calls=%fused_computation.61 | loop fusion | flops 4718592 | bytes 7077904 | tf_op jit(solution)/shard_map/convert_element_type | solution.py:731
  187.4 21.1 %attend_back.1.g_ref = bf16[3,1024,768]{2,1,0:T(8,128)(2,1)} custom-call(bf16[3,1024,768]{2,1,0:T(8,128)(2,1)} %get-tuple-element.119.q_ref.k_ref.v_ref, bf16[3,1024,768]{2,1,0:T(8,128)(2,1)} %get-tuple-element.119.q_ref.k_ref.v_ref, bf16[3,1024,768]{2,1,0:T(8,128)(2,1)} %get-tuple-element.119.q_ref.k_ref.v_ref, ...), custom_call_target="tpu_custom_call" | custom-call | flops 261724569600 | bytes 1061683200 | tf_op jit(solution)/shard_map/attend_back/pallas_call | solution.py:293
  208.5 1.8 fusion.31
  210.3 2.1 fusion.7
  212.5 1.5 collective-permute-start.34
  214.0 8.8 %weight_back.1 = (bf16[3,4,96,768]{3,2,1,0:T(8,128)(2,1)}, bf16[3,4,96,768]{3,2,1,0:T(8,128)(2,1)}, f32[16,768]{1,0:T(8,128)}) custom-call(s32[3]{0:T(128)} %pad_add_fusion.place, bf16[1024,768]{1,0:T(8,128)(2,1)} %fusion.5.x_ref, bf16[3,1024,768]{2,1,0:T(8,128)(2,1)} %attend_back.1.g_ref, f32[8,768]{1,0:T(8,128)} %get-tuple-element.156.vec_in), custom_call_target="tpu_custom_call" | custom-call | flops 181193932800 | bytes 491520000 | tf_op jit(solution)/shard_map/weight_back/pallas_call | solution.py:629
  222.7 1.5 collective-permute-done.34
  224.9 1.7 add_convert_fusion
  231.6 9.6 %input_back.1 = (bf16[1024,768]{1,0:T(8,128)(2,1)}, f32[8,768]{1,0:T(8,128)}) custom-call(bf16[3,1024,768]{2,1,0:T(8,128)(2,1)} %attend_back.1.g_ref, bf16[3,768,768]{2,1,0:T(8,128)(2,1)} %get-tuple-element.162.w_ref, bf16[1024,768]{1,0:T(8,128)(2,1)} %t_ref.3, f32[1024,768]{1,0:T(8,128)} %get-tuple-element.163.mg_ref, ...), custom_call_target="tpu_custom_call" | custom-call | flops 181193932800 | bytes 727449600 | tf_op jit(solution)/shard_map/input_back/pallas_call | solution.py:672
  241.3 2.3 collective-permute-done.37
  243.6 2.1 fusion.9
  245.7 1.5 collective-permute-start.39
  248.1 3.0 %collective-permute-start.44 = (bf16[120,768]{1,0:T(8,128)(2,1)S(1)}, bf16[120,768]{1,0:T(8,128)(2,1)S(1)}, u32[]{:S(2)}, u32[]{:S(2)}) collective-permute-start(bf16[120,768]{1,0:T(8,128)(2,1)S(1)} %fusion.25), channel_id=1, source_target_pairs={{0,4},{1,5},{2,6},{3,7},{4,0},{5,1},{6,2},{7,3},{8,12},{9,13},{10,... | collective-permute-start | bytes 552968 | tf_op jit(solution)/shard_map/ppermute | solution.py:701
  254.3 1.5 fusion.21
  256.8 2.1 collective-permute-done.44
  260.7 3.4 %collective-permute-done.42 = bf16[2,80,768]{2,1,0:T(8,128)(2,1)S(1)} collective-permute-done((bf16[2,80,768]{2,1,0:T(8,128)(2,1)S(1)}, bf16[2,80,768]{2,1,0:T(8,128)(2,1)S(1)}, u32[]{:S(2)}, u32[]{:S(2)}) %collective-permute-start.42) | collective-permute-done | bytes 245792 | tf_op jit(solution)/shard_map/ppermute | solution.py:701
  264.1 3.0 %collective-permute-done.45 = bf16[216,768]{1,0:T(8,128)(2,1)S(1)} collective-permute-done((bf16[216,768]{1,0:T(8,128)(2,1)S(1)}, bf16[216,768]{1,0:T(8,128)(2,1)S(1)}, u32[]{:S(2)}, u32[]{:S(2)}) %collective-permute-start.45) | collective-permute-done | bytes 331808 | tf_op jit(solution)/shard_map/ppermute | solution.py:706
  268.0 1.6 collective-permute-start.43
  269.5 5.5 %collective-permute-done.43 = bf16[80,768]{1,0:T(8,128)(2,1)S(1)} collective-permute-done((bf16[80,768]{1,0:T(8,128)(2,1)S(1)}, bf16[80,768]{1,0:T(8,128)(2,1)S(1)}, u32[]{:S(2)}, u32[]{:S(2)}) %collective-permute-start.43) | collective-permute-done | bytes 122912 | tf_op jit(solution)/shard_map/ppermute | solution.py:701
  275.1 2.8 collective-permute-done.46
  278.6 1.5 collective-permute-start.48
  285.2 2.6 mul.105
  (275 shorter events, 64.7 us)
Async XLA Ops:
  2.3 14.8 %collective-permute-start = (bf16[72,768]{1,0:T(8,128)(2,1)S(1)}, bf16[72,768]{1,0:T(8,128)(2,1)S(1)}, u32[]{:S(2)}, u32[]{:S(2)}) collective-permute-start(bf16[72,768]{1,0:T(8,128)(2,1)S(1)} %pad_maximum_fusion.22), channel_id=1, source_target_pairs={{0,2},{1,3},{2,0},{3,1},{4,6},{5,7},{6,4},{7,5},{8,10},{9,11},{10,... | collective-permute-start | bytes 331784 | tf_op jit(solution)/shard_map/ppermute | solution.py:701
  5.4 11.7 %collective-permute-start.1 = (bf16[72,768]{1,0:T(8,128)(2,1)S(1)}, bf16[72,768]{1,0:T(8,128)(2,1)}, u32[]{:S(2)}, u32[]{:S(2)}) collective-permute-start(bf16[72,768]{1,0:T(8,128)(2,1)S(1)} %pad_maximum_fusion.22), channel_id=1, source_target_pairs={{0,4},{1,5},{2,6},{3,7},{4,0},{5,1},{6,2},{7,3},{8,12},{9,13},{10,... | collective-permute-start | bytes 331784 | tf_op jit(solution)/shard_map/ppermute | solution.py:701
  8.0 9.1 %collective-permute-start.2 = (bf16[72,768]{1,0:T(8,128)(2,1)S(1)}, bf16[72,768]{1,0:T(8,128)(2,1)}, u32[]{:S(2)}, u32[]{:S(2)}) collective-permute-start(bf16[72,768]{1,0:T(8,128)(2,1)S(1)} %pad_maximum_fusion.22), channel_id=1, source_target_pairs={{0,6},{1,7},{2,4},{3,5},{4,2},{5,3},{6,0},{7,1},{8,14},{9,15},{10,... | collective-permute-start | bytes 331784 | tf_op jit(solution)/shard_map/ppermute | solution.py:701
  9.9 41.1 %collective-permute-start.12 = (bf16[3,96,768]{2,1,0:T(8,128)(2,1)}, bf16[3,96,768]{2,1,0:T(8,128)(2,1)}, u32[]{:S(2)}, u32[]{:S(2)}) collective-permute-start(bf16[3,96,768]{2,1,0:T(8,128)(2,1)} %pad_maximum_fusion.12.refs_0_), channel_id=1, source_target_pairs={{0,1},{1,0},{2,3},{3,2},{4,5},{5,4},{6,7},{7,6},{8,9},{9,8},{10,11... | collective-permute-start | bytes 1327112 | tf_op jit(solution)/shard_map/ppermute | solution.py:701
  18.9 7.3 %collective-permute-start.4 = (bf16[3,72,768]{2,1,0:T(8,128)(2,1)}, bf16[3,72,768]{2,1,0:T(8,128)(2,1)S(1)}, u32[]{:S(2)}, u32[]{:S(2)}) collective-permute-start(bf16[3,72,768]{2,1,0:T(8,128)(2,1)} %get-tuple-element.230.refs_1_), channel_id=1, source_target_pairs={{0,8},{1,17},{2,10},{3,19},{4,12},{5,21},{6,14},{7,23},{8,0},{9,25... | collective-permute-start | bytes 995336 | tf_op jit(solution)/shard_map/ppermute | solution.py:706
  20.6 28.1 %collective-permute-start.13 = (bf16[3,72,768]{2,1,0:T(8,128)(2,1)}, bf16[3,72,768]{2,1,0:T(8,128)(2,1)}, u32[]{:S(2)}, u32[]{:S(2)}) collective-permute-start(bf16[3,72,768]{2,1,0:T(8,128)(2,1)} %get-tuple-element.230.refs_1_), channel_id=1, source_target_pairs={{0,1},{1,0},{2,3},{3,2},{4,5},{5,4},{6,7},{7,6},{8,9},{9,8},{10,11... | collective-permute-start | bytes 995336 | tf_op jit(solution)/shard_map/ppermute | solution.py:701
  21.1 3.8 %collective-permute-start.9 = (bf16[8,768]{1,0:T(8,128)(2,1)S(1)}, bf16[8,768]{1,0:T(8,128)(2,1)S(1)}, u32[]{:S(2)}, u32[]{:S(2)}) collective-permute-start(bf16[8,768]{1,0:T(8,128)(2,1)S(1)} %reshape.255), channel_id=1, source_target_pairs={{0,1},{1,0},{2,3},{3,2},{4,5},{5,4},{6,7},{7,6},{8,9},{9,8},{10,11... | collective-permute-start | bytes 36872 | tf_op jit(solution)/shard_map/ppermute | solution.py:701
  22.3 12.5 %collective-permute-start.3 = (bf16[120,768]{1,0:T(8,128)(2,1)S(1)}, bf16[120,768]{1,0:T(8,128)(2,1)S(1)}, u32[]{:S(2)}, u32[]{:S(2)}) collective-permute-start(bf16[120,768]{1,0:T(8,128)(2,1)S(1)} %pad_maximum_fusion.21), channel_id=1, source_target_pairs={{0,4},{1,5},{2,6},{3,7},{4,0},{5,1},{6,2},{7,3},{8,12},{9,13},{10,... | collective-permute-start | bytes 552968 | tf_op jit(solution)/shard_map/ppermute | solution.py:701
  26.3 8.8 %collective-permute-start.10 = (bf16[16,768]{1,0:T(8,128)(2,1)S(1)}, bf16[16,768]{1,0:T(8,128)(2,1)S(1)}, u32[]{:S(2)}, u32[]{:S(2)}) collective-permute-start(bf16[16,768]{1,0:T(8,128)(2,1)S(1)} %pad_maximum_fusion.25), channel_id=1, source_target_pairs={{0,4},{1,5},{2,6},{3,7},{4,0},{5,1},{6,2},{7,3},{8,12},{9,13},{10,... | collective-permute-start | bytes 73736 | tf_op jit(solution)/shard_map/ppermute | solution.py:701
  30.6 10.8 %collective-permute-start.6 = (bf16[2,3,72,768]{3,2,1,0:T(8,128)(2,1)S(1)}, bf16[2,3,72,768]{3,2,1,0:T(8,128)(2,1)}, u32[]{:S(2)}, u32[]{:S(2)}) collective-permute-start(bf16[2,3,72,768]{3,2,1,0:T(8,128)(2,1)S(1)} %pad_maximum_fusion.8), channel_id=1, source_target_pairs={{0,16},{1,9},{2,18},{3,11},{4,20},{5,13},{6,22},{7,15},{8,24},{9,1... | collective-permute-start | bytes 1990664 | tf_op jit(solution)/shard_map/ppermute | solution.py:706
  35.1 4.6 %collective-permute-start.11 = (bf16[2,16,768]{2,1,0:T(8,128)(2,1)S(1)}, bf16[2,16,768]{2,1,0:T(8,128)(2,1)S(1)}, u32[]{:S(2)}, u32[]{:S(2)}) collective-permute-start(bf16[2,16,768]{2,1,0:T(8,128)(2,1)S(1)} %pad_maximum_fusion.24), channel_id=1, source_target_pairs={{0,2},{1,3},{2,0},{3,1},{4,6},{5,7},{6,4},{7,5},{8,10},{9,11},{10,... | collective-permute-start | bytes 147464 | tf_op jit(solution)/shard_map/ppermute | solution.py:701
  35.3 10.8 %collective-permute-start.5 = (bf16[2,120,768]{2,1,0:T(8,128)(2,1)S(1)}, bf16[2,120,768]{2,1,0:T(8,128)(2,1)S(1)}, u32[]{:S(2)}, u32[]{:S(2)}) collective-permute-start(bf16[2,120,768]{2,1,0:T(8,128)(2,1)S(1)} %pad_maximum_fusion.14), channel_id=1, source_target_pairs={{0,2},{1,3},{2,0},{3,1},{4,6},{5,7},{6,4},{7,5},{8,10},{9,11},{10,... | collective-permute-start | bytes 1105928 | tf_op jit(solution)/shard_map/ppermute | solution.py:701
  39.7 11.3 %collective-permute-start.14 = (bf16[3,72,768]{2,1,0:T(8,128)(2,1)}, bf16[3,72,768]{2,1,0:T(8,128)(2,1)}, u32[]{:S(2)}, u32[]{:S(2)}) collective-permute-start(bf16[3,72,768]{2,1,0:T(8,128)(2,1)} %copy-done.23), channel_id=1, source_target_pairs={{0,1},{1,0},{2,3},{3,2},{4,5},{5,4},{6,7},{7,6},{8,9},{9,8},{10,11... | collective-permute-start | bytes 995336 | tf_op jit(solution)/shard_map/ppermute | solution.py:701
  41.4 9.6 %collective-permute-start.15 = (bf16[2,3,72,768]{3,2,1,0:T(8,128)(2,1)}, bf16[2,3,72,768]{3,2,1,0:T(8,128)(2,1)S(1)}, u32[]{:S(2)}, u32[]{:S(2)}) collective-permute-start(bf16[2,3,72,768]{3,2,1,0:T(8,128)(2,1)} %collective-permute-done.6.refs_3_), channel_id=1, source_target_pairs={{0,1},{1,0},{2,3},{3,2},{4,5},{5,4},{6,7},{7,6},{8,9},{9,8},{10,11... | collective-permute-start | bytes 1990664 | tf_op jit(solution)/shard_map/ppermute | solution.py:701
  47.0 14.5 %collective-permute-start.7 = (bf16[3,120,768]{2,1,0:T(8,128)(2,1)}, bf16[3,120,768]{2,1,0:T(8,128)(2,1)}, u32[]{:S(2)}, u32[]{:S(2)}) collective-permute-start(bf16[3,120,768]{2,1,0:T(8,128)(2,1)} %pad_maximum_fusion.10.refs_1_), channel_id=1, source_target_pairs={{0,8},{1,17},{2,10},{3,19},{4,12},{5,21},{6,14},{7,23},{8,0},{9,25... | collective-permute-start | bytes 1658888 | tf_op jit(solution)/shard_map/ppermute | solution.py:706
  48.6 12.9 %collective-permute-start.8 = (bf16[96,768]{1,0:T(8,128)(2,1)}, bf16[96,768]{1,0:T(8,128)(2,1)}, u32[]{:S(2)}, u32[]{:S(2)}) collective-permute-start(bf16[96,768]{1,0:T(8,128)(2,1)} %dynamic-slice_bitcast_fusion.4), channel_id=1, source_target_pairs={{0,4},{1,5},{2,6},{3,7},{4,0},{5,1},{6,2},{7,3},{8,12},{9,13},{10,... | collective-permute-start | bytes 442376 | tf_op jit(solution)/shard_map/ppermute | solution.py:701
  62.7 20.5 %collective-permute-start.17 = (bf16[2,96,768]{2,1,0:T(8,128)(2,1)S(1)}, bf16[2,96,768]{2,1,0:T(8,128)(2,1)S(1)}, u32[]{:S(2)}, u32[]{:S(2)}) collective-permute-start(bf16[2,96,768]{2,1,0:T(8,128)(2,1)S(1)} %pad_maximum_fusion.18), channel_id=1, source_target_pairs={{0,2},{1,3},{2,0},{3,1},{4,6},{5,7},{6,4},{7,5},{8,10},{9,11},{10,... | collective-permute-start | bytes 884744 | tf_op jit(solution)/shard_map/ppermute | solution.py:701
  65.3 17.9 %collective-permute-start.16 = (bf16[2,3,120,768]{3,2,1,0:T(8,128)(2,1)S(1)}, bf16[2,3,120,768]{3,2,1,0:T(8,128)(2,1)S(1)}, u32[]{:S(2)}, u32[]{:S(2)}) collective-permute-start(bf16[2,3,120,768]{3,2,1,0:T(8,128)(2,1)S(1)} %pad_maximum_fusion.5), channel_id=1, source_target_pairs={{0,16},{1,9},{2,18},{3,11},{4,20},{5,13},{6,22},{7,15},{8,24},{9,1... | collective-permute-start | bytes 3317768 | tf_op jit(solution)/shard_map/ppermute | solution.py:706
  66.3 21.4 %collective-permute-start.19 = (bf16[9,96,768]{2,1,0:T(8,128)(2,1)S(1)}, bf16[9,96,768]{2,1,0:T(8,128)(2,1)S(1)}, u32[]{:S(2)}, u32[]{:S(2)}) collective-permute-start(bf16[9,96,768]{2,1,0:T(8,128)(2,1)S(1)} %copy-done.16), channel_id=1, source_target_pairs={{0,1},{1,0},{2,3},{3,2},{4,5},{5,4},{6,7},{7,6},{8,9},{9,8},{10,11... | collective-permute-start | bytes 3981320 | tf_op jit(solution)/shard_map/ppermute | solution.py:701
  83.2 4.5 %collective-permute-start.22 = (bf16[2,3,120,768]{3,2,1,0:T(8,128)(2,1)S(1)}, bf16[2,3,120,768]{3,2,1,0:T(8,128)(2,1)S(1)}, u32[]{:S(2)}, u32[]{:S(2)}) collective-permute-start(bf16[2,3,120,768]{3,2,1,0:T(8,128)(2,1)S(1)} %collective-permute-done.16.refs_3_), channel_id=1, source_target_pairs={{0,1},{1,0},{2,3},{3,2},{4,5},{5,4},{6,7},{7,6},{8,9},{9,8},{10,11... | collective-permute-start | bytes 3317768 | tf_op jit(solution)/shard_map/ppermute | solution.py:701
  83.7 3.2 %collective-permute-start.20 = (bf16[3,120,768]{2,1,0:T(8,128)(2,1)}, bf16[3,120,768]{2,1,0:T(8,128)(2,1)S(1)}, u32[]{:S(2)}, u32[]{:S(2)}) collective-permute-start(bf16[3,120,768]{2,1,0:T(8,128)(2,1)} %pad_maximum_fusion.10.refs_1_), channel_id=1, source_target_pairs={{0,1},{1,0},{2,3},{3,2},{4,5},{5,4},{6,7},{7,6},{8,9},{9,8},{10,11... | collective-permute-start | bytes 1658888 | tf_op jit(solution)/shard_map/ppermute | solution.py:701
  83.8 3.9 %collective-permute-start.21 = (bf16[3,120,768]{2,1,0:T(8,128)(2,1)}, bf16[3,120,768]{2,1,0:T(8,128)(2,1)S(1)}, u32[]{:S(2)}, u32[]{:S(2)}) collective-permute-start(bf16[3,120,768]{2,1,0:T(8,128)(2,1)} %collective-permute-done.7.refs_2_), channel_id=1, source_target_pairs={{0,1},{1,0},{2,3},{3,2},{4,5},{5,4},{6,7},{7,6},{8,9},{9,8},{10,11... | collective-permute-start | bytes 1658888 | tf_op jit(solution)/shard_map/ppermute | solution.py:701
  85.2 12.0 %collective-permute-start.18 = (bf16[3,96,768]{2,1,0:T(8,128)(2,1)S(1)}, bf16[3,96,768]{2,1,0:T(8,128)(2,1)S(1)}, u32[]{:S(2)}, u32[]{:S(2)}) collective-permute-start(bf16[3,96,768]{2,1,0:T(8,128)(2,1)S(1)} %pad_maximum_fusion.13.refs_3_), channel_id=1, source_target_pairs={{0,8},{1,17},{2,10},{3,19},{4,12},{5,21},{6,14},{7,23},{8,0},{9,25... | collective-permute-start | bytes 1327112 | tf_op jit(solution)/shard_map/ppermute | solution.py:706
  98.3 27.0 %collective-permute-start.23 = (bf16[2,3,96,768]{3,2,1,0:T(8,128)(2,1)}, bf16[2,3,96,768]{3,2,1,0:T(8,128)(2,1)}, u32[]{:S(2)}, u32[]{:S(2)}) collective-permute-start(bf16[2,3,96,768]{3,2,1,0:T(8,128)(2,1)} %pad_maximum_fusion.6), channel_id=1, source_target_pairs={{0,16},{1,9},{2,18},{3,11},{4,20},{5,13},{6,22},{7,15},{8,24},{9,1... | collective-permute-start | bytes 2654216 | tf_op jit(solution)/shard_map/ppermute | solution.py:706
  125.3 4.9 %collective-permute-start.24 = (bf16[4,4,96,768]{3,2,1,0:T(8,128)(2,1)}, bf16[4,4,96,768]{3,2,1,0:T(8,128)(2,1)S(1)}, u32[]{:S(2)}, u32[]{:S(2)}) collective-permute-start(bf16[4,4,96,768]{3,2,1,0:T(8,128)(2,1)} %get-tuple-element.136), channel_id=1, source_target_pairs={{0,1},{1,0},{2,3},{3,2},{4,5},{5,4},{6,7},{7,6},{8,9},{9,8},{10,11... | collective-permute-start | bytes 7077896 | tf_op jit(solution)/shard_map/ppermute | solution.py:701
  125.8 8.7 %collective-permute-start.27 = (bf16[2,3,96,768]{3,2,1,0:T(8,128)(2,1)}, bf16[2,3,96,768]{3,2,1,0:T(8,128)(2,1)}, u32[]{:S(2)}, u32[]{:S(2)}) collective-permute-start(bf16[2,3,96,768]{3,2,1,0:T(8,128)(2,1)} %collective-permute-done.23.refs_5_), channel_id=1, source_target_pairs={{0,1},{1,0},{2,3},{3,2},{4,5},{5,4},{6,7},{7,6},{8,9},{9,8},{10,11... | collective-permute-start | bytes 2654216 | tf_op jit(solution)/shard_map/ppermute | solution.py:701
  125.9 8.6 %collective-permute-start.25 = (bf16[3,96,768]{2,1,0:T(8,128)(2,1)S(1)}, bf16[3,96,768]{2,1,0:T(8,128)(2,1)S(1)}, u32[]{:S(2)}, u32[]{:S(2)}) collective-permute-start(bf16[3,96,768]{2,1,0:T(8,128)(2,1)S(1)} %copy-done.12), channel_id=1, source_target_pairs={{0,1},{1,0},{2,3},{3,2},{4,5},{5,4},{6,7},{7,6},{8,9},{9,8},{10,11... | collective-permute-start | bytes 1327112 | tf_op jit(solution)/shard_map/ppermute | solution.py:701
  126.3 8.2 %collective-permute-start.26 = (bf16[3,96,768]{2,1,0:T(8,128)(2,1)}, bf16[3,96,768]{2,1,0:T(8,128)(2,1)}, u32[]{:S(2)}, u32[]{:S(2)}) collective-permute-start(bf16[3,96,768]{2,1,0:T(8,128)(2,1)} %copy-done.22), channel_id=1, source_target_pairs={{0,1},{1,0},{2,3},{3,2},{4,5},{5,4},{6,7},{7,6},{8,9},{9,8},{10,11... | collective-permute-start | bytes 1327112 | tf_op jit(solution)/shard_map/ppermute | solution.py:701
  133.7 29.0 %collective-permute-start.28 = (bf16[2,4,96,768]{3,2,1,0:T(8,128)(2,1)}, bf16[2,4,96,768]{3,2,1,0:T(8,128)(2,1)}, u32[]{:S(2)}, u32[]{:S(2)}) collective-permute-start(bf16[2,4,96,768]{3,2,1,0:T(8,128)(2,1)} %pad_maximum_fusion.4), channel_id=1, source_target_pairs={{0,8},{1,17},{2,10},{3,19},{4,12},{5,21},{6,14},{7,23},{8,0},{9,25... | collective-permute-start | bytes 3538952 | tf_op jit(solution)/shard_map/ppermute | solution.py:706
  162.6 19.4 %collective-permute-start.30 = (bf16[4,4,96,768]{3,2,1,0:T(8,128)(2,1)}, bf16[4,4,96,768]{3,2,1,0:T(8,128)(2,1)}, u32[]{:S(2)}, u32[]{:S(2)}) collective-permute-start(bf16[4,4,96,768]{3,2,1,0:T(8,128)(2,1)} %get-tuple-element.148), channel_id=1, source_target_pairs={{0,1},{1,0},{2,3},{3,2},{4,5},{5,4},{6,7},{7,6},{8,9},{9,8},{10,11... | collective-permute-start | bytes 7077896 | tf_op jit(solution)/shard_map/ppermute | solution.py:701
  164.2 13.6 %collective-permute-start.29 = (bf16[4,96,768]{2,1,0:T(8,128)(2,1)S(1)}, bf16[4,96,768]{2,1,0:T(8,128)(2,1)}, u32[]{:S(2)}, u32[]{:S(2)}) collective-permute-start(bf16[4,96,768]{2,1,0:T(8,128)(2,1)S(1)} %fusion.15), channel_id=1, source_target_pairs={{0,16},{1,9},{2,18},{3,11},{4,20},{5,13},{6,22},{7,15},{8,24},{9,1... | collective-permute-start | bytes 1769480 | tf_op jit(solution)/shard_map/ppermute | solution.py:706
  177.6 3.5 %collective-permute-start.31 = (bf16[1,4,96,768]{3,2,1,0:T(8,128)(2,1)}, bf16[1,4,96,768]{3,2,1,0:T(8,128)(2,1)S(1)}, u32[]{:S(2)}, u32[]{:S(2)}) collective-permute-start(bf16[1,4,96,768]{3,2,1,0:T(8,128)(2,1)} %get-tuple-element.149), channel_id=1, source_target_pairs={{0,1},{1,0},{2,3},{3,2},{4,5},{5,4},{6,7},{7,6},{8,9},{9,8},{10,11... | collective-permute-start | bytes 1769480 | tf_op jit(solution)/shard_map/ppermute | solution.py:701
  180.3 28.1 %collective-permute-start.32 = (bf16[2,96,768]{2,1,0:T(8,128)(2,1)}, bf16[2,96,768]{2,1,0:T(8,128)(2,1)}, u32[]{:S(2)}, u32[]{:S(2)}) collective-permute-start(bf16[2,96,768]{2,1,0:T(8,128)(2,1)} %pad_maximum_fusion.19), channel_id=1, source_target_pairs={{0,2},{1,3},{2,0},{3,1},{4,6},{5,7},{6,4},{7,5},{8,10},{9,11},{10,... | collective-permute-start | bytes 884744 | tf_op jit(solution)/shard_map/ppermute | solution.py:701
  186.7 23.6 %collective-permute-start.33 = (bf16[2,4,120,768]{3,2,1,0:T(8,128)(2,1)}, bf16[2,4,120,768]{3,2,1,0:T(8,128)(2,1)}, u32[]{:S(2)}, u32[]{:S(2)}) collective-permute-start(bf16[2,4,120,768]{3,2,1,0:T(8,128)(2,1)} %pad_maximum_fusion.1), channel_id=1, source_target_pairs={{0,8},{1,17},{2,10},{3,19},{4,12},{5,21},{6,14},{7,23},{8,0},{9,25... | collective-permute-start | bytes 4423688 | tf_op jit(solution)/shard_map/ppermute | solution.py:706
  210.2 12.5 %collective-permute-start.35 = (bf16[96,768]{1,0:T(8,128)(2,1)}, bf16[96,768]{1,0:T(8,128)(2,1)}, u32[]{:S(2)}, u32[]{:S(2)}) collective-permute-start(bf16[96,768]{1,0:T(8,128)(2,1)} %get-tuple-element.208), channel_id=1, source_target_pairs={{0,4},{1,5},{2,6},{3,7},{4,0},{5,1},{6,2},{7,3},{8,12},{9,13},{10,... | collective-permute-start | bytes 442376 | tf_op jit(solution)/shard_map/ppermute | solution.py:701
  212.5 11.8 %collective-permute-start.34 = (bf16[4,120,768]{2,1,0:T(8,128)(2,1)}, bf16[4,120,768]{2,1,0:T(8,128)(2,1)}, u32[]{:S(2)}, u32[]{:S(2)}) collective-permute-start(bf16[4,120,768]{2,1,0:T(8,128)(2,1)} %fusion.7), channel_id=1, source_target_pairs={{0,16},{1,9},{2,18},{3,11},{4,20},{5,13},{6,22},{7,15},{8,24},{9,1... | collective-permute-start | bytes 2211848 | tf_op jit(solution)/shard_map/ppermute | solution.py:706
  224.3 4.5 %collective-permute-start.36 = (bf16[3,4,96,768]{3,2,1,0:T(8,128)(2,1)}, bf16[3,4,96,768]{3,2,1,0:T(8,128)(2,1)S(1)}, u32[]{:S(2)}, u32[]{:S(2)}) collective-permute-start(bf16[3,4,96,768]{3,2,1,0:T(8,128)(2,1)} %get-tuple-element.159), channel_id=1, source_target_pairs={{0,1},{1,0},{2,3},{3,2},{4,5},{5,4},{6,7},{7,6},{8,9},{9,8},{10,11... | collective-permute-start | bytes 5308424 | tf_op jit(solution)/shard_map/ppermute | solution.py:701
  227.6 13.7 %collective-permute-start.38 = (bf16[2,120,768]{2,1,0:T(8,128)(2,1)}, bf16[2,120,768]{2,1,0:T(8,128)(2,1)}, u32[]{:S(2)}, u32[]{:S(2)}) collective-permute-start(bf16[2,120,768]{2,1,0:T(8,128)(2,1)} %pad_maximum_fusion.15), channel_id=1, source_target_pairs={{0,2},{1,3},{2,0},{3,1},{4,6},{5,7},{6,4},{7,5},{8,10},{9,11},{10,... | collective-permute-start | bytes 1105928 | tf_op jit(solution)/shard_map/ppermute | solution.py:701
  230.2 13.4 %collective-permute-start.37 = (bf16[2,3,4,24,768]{4,3,2,1,0:T(8,128)(2,1)}, bf16[2,3,4,24,768]{4,3,2,1,0:T(8,128)(2,1)}, u32[]{:S(2)}, u32[]{:S(2)}) collective-permute-start(bf16[2,3,4,24,768]{4,3,2,1,0:T(8,128)(2,1)} %pad_maximum_fusion.7), channel_id=1, source_target_pairs={{0,8},{1,17},{2,10},{3,19},{4,12},{5,21},{6,14},{7,23},{8,0},{9,25... | collective-permute-start | bytes 2654216 | tf_op jit(solution)/shard_map/ppermute | solution.py:706
  245.7 8.6 %collective-permute-start.39 = (bf16[3,4,24,768]{3,2,1,0:T(8,128)(2,1)}, bf16[3,4,24,768]{3,2,1,0:T(8,128)(2,1)}, u32[]{:S(2)}, u32[]{:S(2)}) collective-permute-start(bf16[3,4,24,768]{3,2,1,0:T(8,128)(2,1)} %fusion.9), channel_id=1, source_target_pairs={{0,16},{1,9},{2,18},{3,11},{4,20},{5,13},{6,22},{7,15},{8,24},{9,1... | collective-permute-start | bytes 1327112 | tf_op jit(solution)/shard_map/ppermute | solution.py:706
  248.1 10.8 %collective-permute-start.44 = (bf16[120,768]{1,0:T(8,128)(2,1)S(1)}, bf16[120,768]{1,0:T(8,128)(2,1)S(1)}, u32[]{:S(2)}, u32[]{:S(2)}) collective-permute-start(bf16[120,768]{1,0:T(8,128)(2,1)S(1)} %fusion.25), channel_id=1, source_target_pairs={{0,4},{1,5},{2,6},{3,7},{4,0},{5,1},{6,2},{7,3},{8,12},{9,13},{10,... | collective-permute-start | bytes 552968 | tf_op jit(solution)/shard_map/ppermute | solution.py:701
  255.9 8.2 %collective-permute-start.42 = (bf16[2,80,768]{2,1,0:T(8,128)(2,1)S(1)}, bf16[2,80,768]{2,1,0:T(8,128)(2,1)S(1)}, u32[]{:S(2)}, u32[]{:S(2)}) collective-permute-start(bf16[2,80,768]{2,1,0:T(8,128)(2,1)S(1)} %pad_maximum_fusion.20), channel_id=1, source_target_pairs={{0,2},{1,3},{2,0},{3,1},{4,6},{5,7},{6,4},{7,5},{8,10},{9,11},{10,... | collective-permute-start | bytes 737288 | tf_op jit(solution)/shard_map/ppermute | solution.py:701
  260.0 7.2 %collective-permute-start.45 = (bf16[216,768]{1,0:T(8,128)(2,1)S(1)}, bf16[216,768]{1,0:T(8,128)(2,1)S(1)}, u32[]{:S(2)}, u32[]{:S(2)}) collective-permute-start(bf16[216,768]{1,0:T(8,128)(2,1)S(1)} %pad_maximum_fusion.17), channel_id=1, source_target_pairs={{0,8},{1,17},{2,10},{3,19},{4,12},{5,21},{6,14},{7,23},{8,0},{9,25... | collective-permute-start | bytes 995336 | tf_op jit(solution)/shard_map/ppermute | solution.py:706
  267.2 10.7 %collective-permute-start.46 = (bf16[2,216,768]{2,1,0:T(8,128)(2,1)S(1)}, bf16[2,216,768]{2,1,0:T(8,128)(2,1)S(1)}, u32[]{:S(2)}, u32[]{:S(2)}) collective-permute-start(bf16[2,216,768]{2,1,0:T(8,128)(2,1)S(1)} %pad_maximum_fusion.9), channel_id=1, source_target_pairs={{0,16},{1,9},{2,18},{3,11},{4,20},{5,13},{6,22},{7,15},{8,24},{9,1... | collective-permute-start | bytes 1990664 | tf_op jit(solution)/shard_map/ppermute | solution.py:706
  268.0 7.1 %collective-permute-start.43 = (bf16[80,768]{1,0:T(8,128)(2,1)S(1)}, bf16[80,768]{1,0:T(8,128)(2,1)S(1)}, u32[]{:S(2)}, u32[]{:S(2)}) collective-permute-start(bf16[80,768]{1,0:T(8,128)(2,1)S(1)} %fusion.33), channel_id=1, source_target_pairs={{0,4},{1,5},{2,6},{3,7},{4,0},{5,1},{6,2},{7,3},{8,12},{9,13},{10,... | collective-permute-start | bytes 368648 | tf_op jit(solution)/shard_map/ppermute | solution.py:701
  278.0 10.6 %collective-permute-start.47 = (bf16[80,768]{1,0:T(8,128)(2,1)S(1)}, bf16[80,768]{1,0:T(8,128)(2,1)S(1)}, u32[]{:S(2)}, u32[]{:S(2)}) collective-permute-start(bf16[80,768]{1,0:T(8,128)(2,1)S(1)} %fusion.23), channel_id=1, source_target_pairs={{0,8},{1,9},{2,10},{3,11},{4,12},{5,13},{6,14},{7,15},{8,0},{9,1},... | collective-permute-start | bytes 368648 | tf_op jit(solution)/shard_map/ppermute | solution.py:701
  278.6 10.0 %collective-permute-start.48 = (bf16[80,768]{1,0:T(8,128)(2,1)S(1)}, bf16[80,768]{1,0:T(8,128)(2,1)S(1)}, u32[]{:S(2)}, u32[]{:S(2)}) collective-permute-start(bf16[80,768]{1,0:T(8,128)(2,1)S(1)} %fusion.23), channel_id=1, source_target_pairs={{0,16},{1,17},{2,18},{3,19},{4,20},{5,21},{6,22},{7,23},{8,24},{9,... | collective-permute-start | bytes 368648 | tf_op jit(solution)/shard_map/ppermute | solution.py:701
  280.1 8.5 %collective-permute-start.49 = (bf16[80,768]{1,0:T(8,128)(2,1)S(1)}, bf16[80,768]{1,0:T(8,128)(2,1)}, u32[]{:S(2)}, u32[]{:S(2)}) collective-permute-start(bf16[80,768]{1,0:T(8,128)(2,1)S(1)} %fusion.23), channel_id=1, source_target_pairs={{0,24},{1,25},{2,26},{3,27},{4,28},{5,29},{6,30},{7,31},{8,16},{9,... | collective-permute-start | bytes 368648 | tf_op jit(solution)/shard_map/ppermute | solution.py:701
  (47 other events, 358.0 us)
where the time goes:
time: 295 us; the launch traced here: 293 us
  Pallas kernels  138 us (47%)
  other arithmetic  48.3 us (16%)
  starting transfers between devices  48.2 us (16%)
  waiting for transfers between devices  36.4 us (12%)
  local copies, waits for them, and re-layouts  20.4 us (7%)
    pallas_call x2, Pallas kernels, ffn_fast_call(): pl.pallas_call(partial(ffn_fast_kernel, start, lead), grid_spec=pltpu.Pre...  53.2 us
    ppermute x36, starting transfers between devices, hop(): return lax.ppermute(x, ('dp', 'fsdp'), [(i, i ^ mask) for i in range(32)])  30.9 us
    ppermute x36, waiting for transfers between devices, hop(): return lax.ppermute(x, ('dp', 'fsdp'), [(i, i ^ mask) for i in range(32)])  23.5 us
    pallas_call x1, Pallas kernels, attn_bwd_call(): pl.pallas_call(attn_bwd_kernel, grid=(seqs, hp), in_specs=[part(0), part(...  21.1 us
    convert_element_type x14, other arithmetic, add_two(): return (wide(a) + wide(b)).astype(bf16)  20.5 us
    ppermute x14, starting transfers between devices, group_hop(): return lax.ppermute(x, ('dp', 'fsdp'), pairs)  17.3 us
    pallas_call x1, Pallas kernels, attn_fwd_call(): pl.pallas_call(attn_fwd_kernel, grid=(seqs, hp), in_specs=[part(0), part(...  16.9 us
    ppermute x14, waiting for transfers between devices, group_hop(): return lax.ppermute(x, ('dp', 'fsdp'), pairs)  12.9 us
  transfers between devices with their start and end apart: 50, of which 17 were waited for; matrix products, arithmetic and copies ran while one was open for 18% of the time, Pallas kernels for 47%

commit v1 on v0

--- a/solution.py
+++ b/solution.py
@@ -692,6 +692,43 @@
     )(grads, w, tokens, mg, table, *([] if start else [before[1], before[0]]))
 
 
+def finish_kernel(factor, order, x_ref, up_ref, down_ref, out_ref):
+    n = up_ref.shape[0]
+    few = n // 4
+    for b in range(4):
+        x = x_ref[order[b]].astype(f32) * factor
+        out_ref[b * few : (b + 1) * few, :] = x[2 * n :]
+        for half in range(2):
+            block, p = x[half * n : (half + 1) * n], 2 * half + b // 2
+            if b % 2:
+                down_ref[p * n : (p + 1) * n, :] = block
+            else:
+                for s in range(8):
+                    to = s * 4 * n + p * n
+                    up_ref[:, to : to + n] = block[:, s * n : (s + 1) * n]
+
+
+def finish_call(order, final, factor):
+    n, d = final.shape[1] * 4 // 9, final.shape[2]
+    full = lambda *shape: pl.BlockSpec(shape, lambda i, order: (0,) * len(shape))
+    return pl.pallas_call(
+        partial(finish_kernel, factor),
+        grid_spec=pltpu.PrefetchScalarGridSpec(
+            num_scalar_prefetch=1,
+            grid=(1,),
+            in_specs=[full(*final.shape)],
+            out_specs=[full(n, 4 * d), full(4 * n, d), full(n, d)],
+        ),
+        out_shape=[
+            jax.ShapeDtypeStruct((n, 4 * d), f32),
+            jax.ShapeDtypeStruct((4 * n, d), f32),
+            jax.ShapeDtypeStruct((n, d), f32),
+        ],
+        compiler_params=params(1),
+        name="finish",
+    )(order, final)
+
+
 CORE = 1
 ALONG = (2, 4, 6)
 GROUP = (8, 16, 24)
@@ -962,12 +999,21 @@
     final_feed = jnp.stack([final_feed, feed_near, feed_far[0], feed_far[1]])
     order = lambda b: jnp.where(b == one, 1, jnp.where(b == two, 2, b))
     final_attn = [pick(final_rest, dp ^ b)[:many].reshape(3, many // 3, d) for b in range(4)]
-    final_feed = [pick(final_feed, order(dp ^ b)) for b in range(4)]
-    attn = [jnp.concatenate([x[i] for x in final_attn]) for i in range(3)]
-    attn.append(jnp.concatenate([x[2 * n :] for x in final_feed]))
-    feed = [x[:n] for x in final_feed] + [x[n : 2 * n] for x in final_feed]
     factor = (32 * rows) ** (-0.5)
-    return outputs(layer_out, input_grad, attn, feed, vec, factor, 8)
+    members = jnp.stack([order(dp ^ b) for b in range(4)]).astype(jnp.int32)
+    up, down, out = finish_call(members, final_feed, factor)
+    vec = vec * factor
+    return (
+        layer_out,
+        input_grad,
+        *(wide(jnp.concatenate([x[i] for x in final_attn])) * factor for i in range(3)),
+        out,
+        up,
+        down,
+        *(vec[i] for i in VEC_ROWS),
+        vec[UP_ROW:].reshape(-1),
+        vec[DOWN_ROW],
+    )
 
 
 def gather(local):

time: 295 us -> 291 us (0.986)
  local copies, waits for them, and re-layouts: 20.4 us -> 14.8 us
  Pallas kernels: 138 us -> 142 us
    pallas_call x0 -> x1, Pallas kernels: none -> 4.03 us  [finish_call(): pl.pallas_call(partial(finish_kernel, factor), grid_spec=pltpu.PrefetchSc...]
    mul x2 -> x0, local copies, waits for them, and re-layouts: 3.66 us -> none  [outputs(): wide(up.reshape(m, parts * d)) * factor]
  transfers between devices with their start and end apart: 50 -> 50, of which waited for: 17 -> 17; matrix products, arithmetic and copies ran while one was open for 18% -> 16% of each run, Pallas kernels for 47% -> 49%
where the time goes in v1:
time: 291 us; the launch traced here: 290 us
  Pallas kernels  142 us (49%)
  starting transfers between devices  48.2 us (17%)
  other arithmetic  46.8 us (16%)
  waiting for transfers between devices  35.8 us (12%)
  local copies, waits for them, and re-layouts  14.8 us (5%)
    pallas_call x2, Pallas kernels, ffn_fast_call(): pl.pallas_call(partial(ffn_fast_kernel, start, lead), grid_spec=pltpu.Pre...  53.2 us
    ppermute x36, starting transfers between devices, hop(): return lax.ppermute(x, ('dp', 'fsdp'), [(i, i ^ mask) for i in range(32)])  30.9 us
    ppermute x36, waiting for transfers between devices, hop(): return lax.ppermute(x, ('dp', 'fsdp'), [(i, i ^ mask) for i in range(32)])  22.9 us
    pallas_call x1, Pallas kernels, attn_bwd_call(): pl.pallas_call(attn_bwd_kernel, grid=(seqs, hp), in_specs=[part(0), part(...  21.1 us
    convert_element_type x14, other arithmetic, add_two(): return (wide(a) + wide(b)).astype(bf16)  20.5 us
    ppermute x14, starting transfers between devices, group_hop(): return lax.ppermute(x, ('dp', 'fsdp'), pairs)  17.2 us
    pallas_call x1, Pallas kernels, attn_fwd_call(): pl.pallas_call(attn_fwd_kernel, grid=(seqs, hp), in_specs=[part(0), part(...  16.9 us
    ppermute x14, waiting for transfers between devices, group_hop(): return lax.ppermute(x, ('dp', 'fsdp'), pairs)  12.9 us
  transfers between devices with their start and end apart: 50, of which 17 were waited for; matrix products, arithmetic and copies ran while one was open for 16% of the time, Pallas kernels for 49%

profile of v1, /device:TPU:0, one launch (start us, length us, event | category | flops | bytes accessed | tf_op | source)
XLA Modules:
  0.0 289.7 jit_solution(1720655885141245601)
XLA Ops:
  2.3 3.1 %collective-permute-start = (bf16[72,768]{1,0:T(8,128)(2,1)S(1)}, bf16[72,768]{1,0:T(8,128)(2,1)S(1)}, u32[]{:S(2)}, u32[]{:S(2)}) collective-permute-start(bf16[72,768]{1,0:T(8,128)(2,1)S(1)} %pad_maximum_fusion.22), channel_id=1, source_target_pairs={{0,2},{1,3},{2,0},{3,1},{4,6},{5,7},{6,4},{7,5},{8,10},{9,11},{10,... | collective-permute-start | bytes 331784 | tf_op jit(solution)/shard_map/ppermute | solution.py:738
  5.4 2.6 collective-permute-start.1
  8.0 1.9 pad_maximum_fusion.12.refs_0_
  17.1 1.7 fusion.39
  18.9 1.7 collective-permute-start.4
  22.3 2.4 collective-permute-start.3
  26.3 2.6 collective-permute-start.10
  30.6 1.5 collective-permute-start.6
  32.1 2.7 collective-permute-done.3
  35.3 1.9 collective-permute-start.5
  37.2 2.5 collective-permute-done.11
  41.4 1.8 fusion.5.x_ref
  43.9 2.2 collective-permute-done.5
  47.0 1.6 collective-permute-start.7
  48.6 2.4 collective-permute-start.8
  51.0 9.7 %qkv.1 = (bf16[3,1024,768]{2,1,0:T(8,128)(2,1)}, bf16[3,768,768]{2,1,0:T(8,128)(2,1)}) custom-call(s32[3]{0:T(128)} %pad_add_fusion.place, bf16[1024,768]{1,0:T(8,128)(2,1)} %fusion.5.x_ref, f32[13,1,768]{2,1,0:T(1,128)} %convert_element_type.460.b_ref.bo_ref.g_ref.s_ref.bd_ref.gain_ref, bf16[3,96,768]{2,1,0:T(8,128)(2,1)} %pad_maximum_fusion.12.refs_0_, ...), custom_call_target="tpu_custom_call" | custom-call | flops 181193932800 | bytes 786432000 | tf_op jit(solution)/shard_map/qkv/pallas_call | solution.py:158
  65.5 16.9 %attend.1 = (bf16[1024,768]{1,0:T(8,128)(2,1)}, bf16[24,2,416,256]{3,2,1,0:T(8,128)(2,1)}) custom-call(bf16[3,1024,768]{2,1,0:T(8,128)(2,1)} %get-tuple-element.122.q_ref.k_ref.v_ref, bf16[3,1024,768]{2,1,0:T(8,128)(2,1)} %get-tuple-element.122.q_ref.k_ref.v_ref, bf16[3,1024,768]{2,1,0:T(8,128)(2,1)} %get-tuple-element.122.q_ref.k_ref.v_ref, ...), custom_call_target="tpu_custom_call" | custom-call | flops 130862284800 | bytes 825753600 | tf_op jit(solution)/shard_map/attend/pallas_call | solution.py:223
  84.4 1.5 collective-permute-start.18
  89.1 7.3 %project.1 = (f32[1024,768]{1,0:T(8,128)}, bf16[1024,768]{1,0:T(8,128)(2,1)}, bf16[1,768,768]{2,1,0:T(8,128)(2,1)}) custom-call(s32[3]{0:T(128)} %pad_add_fusion.place, bf16[1024,768]{1,0:T(8,128)(2,1)} %get-tuple-element.128.a_ref, bf16[1024,768]{1,0:T(8,128)(2,1)} %t_ref.3, f32[13,1,768]{2,1,0:T(1,128)} %convert_element_type.460.b_ref.bo_ref.g_ref.s_ref.bd_ref.gain_ref, ...), custom_call_target="tpu_custom_call" | custom-call | flops 60397977600 | bytes 511180800 | tf_op jit(solution)/shard_map/project/pallas_call | solution.py:341
  98.6 25.9 %feed.2 = (bf16[4,4,96,768]{3,2,1,0:T(8,128)(2,1)}, bf16[4,4,96,768]{3,2,1,0:T(8,128)(2,1)}, f32[8,768]{1,0:T(8,128)}, f32[1024,768]{1,0:T(8,128)}, f32[1024,768]{1,0:T(8,128)}) custom-call(s32[3]{0:T(128)} %pad_add_fusion.place, bf16[1024,768]{1,0:T(8,128)(2,1)} %get-tuple-element.134.x_ref, bf16[1024,768]{1,0:T(8,128)(2,1)} %dy_ref.1, ...), custom_call_target="tpu_custom_call" | custom-call | flops 724775731200 | bytes 1258291200 | tf_op jit(solution)/shard_map/feed/pallas_call | solution.py:483
  125.6 3.8 %collective-permute-done.24 = bf16[4,4,96,768]{3,2,1,0:T(8,128)(2,1)S(1)} collective-permute-done((bf16[4,4,96,768]{3,2,1,0:T(8,128)(2,1)}, bf16[4,4,96,768]{3,2,1,0:T(8,128)(2,1)S(1)}, u32[]{:S(2)}, u32[]{:S(2)}) %collective-permute-start.24) | collective-permute-done | bytes 2359328 | tf_op jit(solution)/shard_map/ppermute | solution.py:738
  129.4 2.4 add_convert_fusion.10
  134.5 27.3 %feed.3 = (bf16[4,4,96,768]{3,2,1,0:T(8,128)(2,1)}, bf16[4,4,96,768]{3,2,1,0:T(8,128)(2,1)}, f32[8,768]{1,0:T(8,128)}, f32[1024,768]{1,0:T(8,128)}, f32[1024,768]{1,0:T(8,128)}) custom-call(s32[3]{0:T(128)} %pad_add_fusion.place, bf16[1024,768]{1,0:T(8,128)(2,1)} %get-tuple-element.134.x_ref, bf16[1024,768]{1,0:T(8,128)(2,1)} %dy_ref.1, ...), custom_call_target="tpu_custom_call" | custom-call | flops 724775731200 | bytes 1258291200 | tf_op jit(solution)/shard_map/feed/pallas_call | solution.py:483
  163.4 1.6 collective-permute-start.29
  164.9 11.9 %middle_back.1 = (f32[1024,768]{1,0:T(8,128)}, bf16[1024,768]{1,0:T(8,128)(2,1)}, f32[8,768]{1,0:T(8,128)}, bf16[1024,768]{1,0:T(8,128)(2,1)}, bf16[1,4,96,768]{...) custom-call(s32[3]{0:T(128)} %pad_add_fusion.place, f32[1024,768]{1,0:T(8,128)} %get-tuple-element.145.sg_ref, ...), custom_call_target="tpu_custom_call" | custom-call | flops 120795955200 | bytes 983040000 | tf_op jit(solution)/shard_map/middle_back/pallas_call | solution.py:558
  176.9 1.8 fusion.8
  181.2 3.3 %fusion.14 = (bf16[4,96,768]{2,1,0:T(8,128)(2,1)}, bf16[4,96,768]{2,1,0:T(8,128)(2,1)S(1)}, bf16[4,96,768]{2,1,0:T(8,128)(2,1)S(1)}, bf16[4,96,768]{2,1,0:T(8,128)(2,1)}) fusion(bf16[4,4,96,768]{3,2,1,0:T(8,128)(2,1)} %collective-permute-done.30, s32[]{:T(128)S(6)} %select_n.161, bf16[4,4,96,768]{3,2,1,0:T(8,128)(2,1)S(1)} %copy-done.5, s32[]{:T(128)S(6)} %select_n.172, ...), kind=kLoop, calls=%fused_computation.59 | loop fusion | flops 4718592 | bytes 7077904 | tf_op jit(solution)/shard_map/convert_element_type | solution.py:768
  186.6 21.1 %attend_back.1.g_ref = bf16[3,1024,768]{2,1,0:T(8,128)(2,1)} custom-call(bf16[3,1024,768]{2,1,0:T(8,128)(2,1)} %get-tuple-element.122.q_ref.k_ref.v_ref, bf16[3,1024,768]{2,1,0:T(8,128)(2,1)} %get-tuple-element.122.q_ref.k_ref.v_ref, bf16[3,1024,768]{2,1,0:T(8,128)(2,1)} %get-tuple-element.122.q_ref.k_ref.v_ref, ...), custom_call_target="tpu_custom_call" | custom-call | flops 261724569600 | bytes 1061683200 | tf_op jit(solution)/shard_map/attend_back/pallas_call | solution.py:293
  207.7 1.8 fusion.31
  209.6 2.1 fusion.7
  211.7 1.5 collective-permute-start.34
  213.2 8.8 %weight_back.1 = (bf16[3,4,96,768]{3,2,1,0:T(8,128)(2,1)}, bf16[3,4,96,768]{3,2,1,0:T(8,128)(2,1)}, f32[16,768]{1,0:T(8,128)}) custom-call(s32[3]{0:T(128)} %pad_add_fusion.place, bf16[1024,768]{1,0:T(8,128)(2,1)} %fusion.5.x_ref, bf16[3,1024,768]{2,1,0:T(8,128)(2,1)} %attend_back.1.g_ref, f32[8,768]{1,0:T(8,128)} %get-tuple-element.159.vec_in), custom_call_target="tpu_custom_call" | custom-call | flops 181193932800 | bytes 491520000 | tf_op jit(solution)/shard_map/weight_back/pallas_call | solution.py:629
  222.0 1.5 collective-permute-done.34
  224.1 1.7 add_convert_fusion
  230.8 9.6 %input_back.1 = (bf16[1024,768]{1,0:T(8,128)(2,1)}, f32[8,768]{1,0:T(8,128)}) custom-call(bf16[3,1024,768]{2,1,0:T(8,128)(2,1)} %attend_back.1.g_ref, bf16[3,768,768]{2,1,0:T(8,128)(2,1)} %get-tuple-element.165.w_ref, bf16[1024,768]{1,0:T(8,128)(2,1)} %t_ref.3, f32[1024,768]{1,0:T(8,128)} %get-tuple-element.166.mg_ref, ...), custom_call_target="tpu_custom_call" | custom-call | flops 181193932800 | bytes 727449600 | tf_op jit(solution)/shard_map/input_back/pallas_call | solution.py:672
  240.5 2.3 collective-permute-done.37
  242.8 2.1 fusion.9
  244.9 1.5 collective-permute-start.39
  247.4 3.0 %collective-permute-start.44 = (bf16[120,768]{1,0:T(8,128)(2,1)S(1)}, bf16[120,768]{1,0:T(8,128)(2,1)S(1)}, u32[]{:S(2)}, u32[]{:S(2)}) collective-permute-start(bf16[120,768]{1,0:T(8,128)(2,1)S(1)} %fusion.25), channel_id=1, source_target_pairs={{0,4},{1,5},{2,6},{3,7},{4,0},{5,1},{6,2},{7,3},{8,12},{9,13},{10,... | collective-permute-start | bytes 552968 | tf_op jit(solution)/shard_map/ppermute | solution.py:738
  253.5 1.5 fusion.21
  256.0 2.1 collective-permute-done.44
  259.9 3.4 %collective-permute-done.42 = bf16[2,80,768]{2,1,0:T(8,128)(2,1)S(1)} collective-permute-done((bf16[2,80,768]{2,1,0:T(8,128)(2,1)S(1)}, bf16[2,80,768]{2,1,0:T(8,128)(2,1)S(1)}, u32[]{:S(2)}, u32[]{:S(2)}) %collective-permute-start.42) | collective-permute-done | bytes 245792 | tf_op jit(solution)/shard_map/ppermute | solution.py:738
  263.4 3.0 %collective-permute-done.45 = bf16[216,768]{1,0:T(8,128)(2,1)S(1)} collective-permute-done((bf16[216,768]{1,0:T(8,128)(2,1)S(1)}, bf16[216,768]{1,0:T(8,128)(2,1)S(1)}, u32[]{:S(2)}, u32[]{:S(2)}) %collective-permute-start.45) | collective-permute-done | bytes 331808 | tf_op jit(solution)/shard_map/ppermute | solution.py:743
  267.2 1.6 collective-permute-start.43
  269.3 4.9 %collective-permute-done.43 = bf16[80,768]{1,0:T(8,128)(2,1)S(1)} collective-permute-done((bf16[80,768]{1,0:T(8,128)(2,1)S(1)}, bf16[80,768]{1,0:T(8,128)(2,1)S(1)}, u32[]{:S(2)}, u32[]{:S(2)}) %collective-permute-start.43) | collective-permute-done | bytes 122912 | tf_op jit(solution)/shard_map/ppermute | solution.py:738
  274.3 2.8 collective-permute-done.46
  277.8 1.5 collective-permute-start.48
  281.9 4.0 %finish.1 = (f32[96,3072]{1,0:T(8,128)}, f32[384,768]{1,0:T(8,128)}, f32[96,768]{1,0:T(8,128)}) custom-call(s32[4]{0:T(128)} %pad_add_fusion.1.order, bf16[4,216,768]{2,1,0:T(8,128)(2,1)} %pad_maximum_fusion.3.x_ref), custom_call_target="tpu_custom_call" | custom-call | tf_op jit(solution)/shard_map/finish/pallas_call | solution.py:714
  (264 shorter events, 60.2 us)
Async XLA Ops:
  2.3 14.8 %collective-permute-start = (bf16[72,768]{1,0:T(8,128)(2,1)S(1)}, bf16[72,768]{1,0:T(8,128)(2,1)S(1)}, u32[]{:S(2)}, u32[]{:S(2)}) collective-permute-start(bf16[72,768]{1,0:T(8,128)(2,1)S(1)} %pad_maximum_fusion.22), channel_id=1, source_target_pairs={{0,2},{1,3},{2,0},{3,1},{4,6},{5,7},{6,4},{7,5},{8,10},{9,11},{10,... | collective-permute-start | bytes 331784 | tf_op jit(solution)/shard_map/ppermute | solution.py:738
  5.4 11.7 %collective-permute-start.1 = (bf16[72,768]{1,0:T(8,128)(2,1)S(1)}, bf16[72,768]{1,0:T(8,128)(2,1)}, u32[]{:S(2)}, u32[]{:S(2)}) collective-permute-start(bf16[72,768]{1,0:T(8,128)(2,1)S(1)} %pad_maximum_fusion.22), channel_id=1, source_target_pairs={{0,4},{1,5},{2,6},{3,7},{4,0},{5,1},{6,2},{7,3},{8,12},{9,13},{10,... | collective-permute-start | bytes 331784 | tf_op jit(solution)/shard_map/ppermute | solution.py:738
  8.0 9.1 %collective-permute-start.2 = (bf16[72,768]{1,0:T(8,128)(2,1)S(1)}, bf16[72,768]{1,0:T(8,128)(2,1)}, u32[]{:S(2)}, u32[]{:S(2)}) collective-permute-start(bf16[72,768]{1,0:T(8,128)(2,1)S(1)} %pad_maximum_fusion.22), channel_id=1, source_target_pairs={{0,6},{1,7},{2,4},{3,5},{4,2},{5,3},{6,0},{7,1},{8,14},{9,15},{10,... | collective-permute-start | bytes 331784 | tf_op jit(solution)/shard_map/ppermute | solution.py:738
  9.9 41.1 %collective-permute-start.12 = (bf16[3,96,768]{2,1,0:T(8,128)(2,1)}, bf16[3,96,768]{2,1,0:T(8,128)(2,1)}, u32[]{:S(2)}, u32[]{:S(2)}) collective-permute-start(bf16[3,96,768]{2,1,0:T(8,128)(2,1)} %pad_maximum_fusion.12.refs_0_), channel_id=1, source_target_pairs={{0,1},{1,0},{2,3},{3,2},{4,5},{5,4},{6,7},{7,6},{8,9},{9,8},{10,11... | collective-permute-start | bytes 1327112 | tf_op jit(solution)/shard_map/ppermute | solution.py:738
  18.9 7.3 %collective-permute-start.4 = (bf16[3,72,768]{2,1,0:T(8,128)(2,1)}, bf16[3,72,768]{2,1,0:T(8,128)(2,1)S(1)}, u32[]{:S(2)}, u32[]{:S(2)}) collective-permute-start(bf16[3,72,768]{2,1,0:T(8,128)(2,1)} %get-tuple-element.224.refs_1_), channel_id=1, source_target_pairs={{0,8},{1,17},{2,10},{3,19},{4,12},{5,21},{6,14},{7,23},{8,0},{9,25... | collective-permute-start | bytes 995336 | tf_op jit(solution)/shard_map/ppermute | solution.py:743
  20.6 28.0 %collective-permute-start.13 = (bf16[3,72,768]{2,1,0:T(8,128)(2,1)}, bf16[3,72,768]{2,1,0:T(8,128)(2,1)}, u32[]{:S(2)}, u32[]{:S(2)}) collective-permute-start(bf16[3,72,768]{2,1,0:T(8,128)(2,1)} %get-tuple-element.224.refs_1_), channel_id=1, source_target_pairs={{0,1},{1,0},{2,3},{3,2},{4,5},{5,4},{6,7},{7,6},{8,9},{9,8},{10,11... | collective-permute-start | bytes 995336 | tf_op jit(solution)/shard_map/ppermute | solution.py:738
  21.1 3.8 %collective-permute-start.9 = (bf16[8,768]{1,0:T(8,128)(2,1)S(1)}, bf16[8,768]{1,0:T(8,128)(2,1)S(1)}, u32[]{:S(2)}, u32[]{:S(2)}) collective-permute-start(bf16[8,768]{1,0:T(8,128)(2,1)S(1)} %reshape.230), channel_id=1, source_target_pairs={{0,1},{1,0},{2,3},{3,2},{4,5},{5,4},{6,7},{7,6},{8,9},{9,8},{10,11... | collective-permute-start | bytes 36872 | tf_op jit(solution)/shard_map/ppermute | solution.py:738
  22.3 12.5 %collective-permute-start.3 = (bf16[120,768]{1,0:T(8,128)(2,1)S(1)}, bf16[120,768]{1,0:T(8,128)(2,1)S(1)}, u32[]{:S(2)}, u32[]{:S(2)}) collective-permute-start(bf16[120,768]{1,0:T(8,128)(2,1)S(1)} %pad_maximum_fusion.21), channel_id=1, source_target_pairs={{0,4},{1,5},{2,6},{3,7},{4,0},{5,1},{6,2},{7,3},{8,12},{9,13},{10,... | collective-permute-start | bytes 552968 | tf_op jit(solution)/shard_map/ppermute | solution.py:738
  26.3 8.8 %collective-permute-start.10 = (bf16[16,768]{1,0:T(8,128)(2,1)S(1)}, bf16[16,768]{1,0:T(8,128)(2,1)S(1)}, u32[]{:S(2)}, u32[]{:S(2)}) collective-permute-start(bf16[16,768]{1,0:T(8,128)(2,1)S(1)} %pad_maximum_fusion.25), channel_id=1, source_target_pairs={{0,4},{1,5},{2,6},{3,7},{4,0},{5,1},{6,2},{7,3},{8,12},{9,13},{10,... | collective-permute-start | bytes 73736 | tf_op jit(solution)/shard_map/ppermute | solution.py:738
  30.6 10.8 %collective-permute-start.6 = (bf16[2,3,72,768]{3,2,1,0:T(8,128)(2,1)S(1)}, bf16[2,3,72,768]{3,2,1,0:T(8,128)(2,1)}, u32[]{:S(2)}, u32[]{:S(2)}) collective-permute-start(bf16[2,3,72,768]{3,2,1,0:T(8,128)(2,1)S(1)} %pad_maximum_fusion.8), channel_id=1, source_target_pairs={{0,16},{1,9},{2,18},{3,11},{4,20},{5,13},{6,22},{7,15},{8,24},{9,1... | collective-permute-start | bytes 1990664 | tf_op jit(solution)/shard_map/ppermute | solution.py:743
  35.1 4.6 %collective-permute-start.11 = (bf16[2,16,768]{2,1,0:T(8,128)(2,1)S(1)}, bf16[2,16,768]{2,1,0:T(8,128)(2,1)S(1)}, u32[]{:S(2)}, u32[]{:S(2)}) collective-permute-start(bf16[2,16,768]{2,1,0:T(8,128)(2,1)S(1)} %pad_maximum_fusion.24), channel_id=1, source_target_pairs={{0,2},{1,3},{2,0},{3,1},{4,6},{5,7},{6,4},{7,5},{8,10},{9,11},{10,... | collective-permute-start | bytes 147464 | tf_op jit(solution)/shard_map/ppermute | solution.py:738
  35.3 10.8 %collective-permute-start.5 = (bf16[2,120,768]{2,1,0:T(8,128)(2,1)S(1)}, bf16[2,120,768]{2,1,0:T(8,128)(2,1)S(1)}, u32[]{:S(2)}, u32[]{:S(2)}) collective-permute-start(bf16[2,120,768]{2,1,0:T(8,128)(2,1)S(1)} %pad_maximum_fusion.14), channel_id=1, source_target_pairs={{0,2},{1,3},{2,0},{3,1},{4,6},{5,7},{6,4},{7,5},{8,10},{9,11},{10,... | collective-permute-start | bytes 1105928 | tf_op jit(solution)/shard_map/ppermute | solution.py:738
  39.7 11.3 %collective-permute-start.14 = (bf16[3,72,768]{2,1,0:T(8,128)(2,1)}, bf16[3,72,768]{2,1,0:T(8,128)(2,1)}, u32[]{:S(2)}, u32[]{:S(2)}) collective-permute-start(bf16[3,72,768]{2,1,0:T(8,128)(2,1)} %copy-done.23), channel_id=1, source_target_pairs={{0,1},{1,0},{2,3},{3,2},{4,5},{5,4},{6,7},{7,6},{8,9},{9,8},{10,11... | collective-permute-start | bytes 995336 | tf_op jit(solution)/shard_map/ppermute | solution.py:738
  41.4 9.6 %collective-permute-start.15 = (bf16[2,3,72,768]{3,2,1,0:T(8,128)(2,1)}, bf16[2,3,72,768]{3,2,1,0:T(8,128)(2,1)}, u32[]{:S(2)}, u32[]{:S(2)}) collective-permute-start(bf16[2,3,72,768]{3,2,1,0:T(8,128)(2,1)} %collective-permute-done.6.refs_3_), channel_id=1, source_target_pairs={{0,1},{1,0},{2,3},{3,2},{4,5},{5,4},{6,7},{7,6},{8,9},{9,8},{10,11... | collective-permute-start | bytes 1990664 | tf_op jit(solution)/shard_map/ppermute | solution.py:738
  47.0 13.7 %collective-permute-start.7 = (bf16[3,120,768]{2,1,0:T(8,128)(2,1)}, bf16[3,120,768]{2,1,0:T(8,128)(2,1)}, u32[]{:S(2)}, u32[]{:S(2)}) collective-permute-start(bf16[3,120,768]{2,1,0:T(8,128)(2,1)} %pad_maximum_fusion.10.refs_1_), channel_id=1, source_target_pairs={{0,8},{1,17},{2,10},{3,19},{4,12},{5,21},{6,14},{7,23},{8,0},{9,25... | collective-permute-start | bytes 1658888 | tf_op jit(solution)/shard_map/ppermute | solution.py:743
  48.6 12.1 %collective-permute-start.8 = (bf16[96,768]{1,0:T(8,128)(2,1)}, bf16[96,768]{1,0:T(8,128)(2,1)}, u32[]{:S(2)}, u32[]{:S(2)}) collective-permute-start(bf16[96,768]{1,0:T(8,128)(2,1)} %dynamic-slice_bitcast_fusion), channel_id=1, source_target_pairs={{0,4},{1,5},{2,6},{3,7},{4,0},{5,1},{6,2},{7,3},{8,12},{9,13},{10,... | collective-permute-start | bytes 442376 | tf_op jit(solution)/shard_map/ppermute | solution.py:738
  61.8 20.5 %collective-permute-start.17 = (bf16[2,96,768]{2,1,0:T(8,128)(2,1)S(1)}, bf16[2,96,768]{2,1,0:T(8,128)(2,1)S(1)}, u32[]{:S(2)}, u32[]{:S(2)}) collective-permute-start(bf16[2,96,768]{2,1,0:T(8,128)(2,1)S(1)} %pad_maximum_fusion.18), channel_id=1, source_target_pairs={{0,2},{1,3},{2,0},{3,1},{4,6},{5,7},{6,4},{7,5},{8,10},{9,11},{10,... | collective-permute-start | bytes 884744 | tf_op jit(solution)/shard_map/ppermute | solution.py:738
  64.5 17.9 %collective-permute-start.16 = (bf16[2,3,120,768]{3,2,1,0:T(8,128)(2,1)S(1)}, bf16[2,3,120,768]{3,2,1,0:T(8,128)(2,1)S(1)}, u32[]{:S(2)}, u32[]{:S(2)}) collective-permute-start(bf16[2,3,120,768]{3,2,1,0:T(8,128)(2,1)S(1)} %pad_maximum_fusion.5), channel_id=1, source_target_pairs={{0,16},{1,9},{2,18},{3,11},{4,20},{5,13},{6,22},{7,15},{8,24},{9,1... | collective-permute-start | bytes 3317768 | tf_op jit(solution)/shard_map/ppermute | solution.py:743
  65.5 21.4 %collective-permute-start.19 = (bf16[9,96,768]{2,1,0:T(8,128)(2,1)S(1)}, bf16[9,96,768]{2,1,0:T(8,128)(2,1)S(1)}, u32[]{:S(2)}, u32[]{:S(2)}) collective-permute-start(bf16[9,96,768]{2,1,0:T(8,128)(2,1)S(1)} %copy-done.16), channel_id=1, source_target_pairs={{0,1},{1,0},{2,3},{3,2},{4,5},{5,4},{6,7},{7,6},{8,9},{9,8},{10,11... | collective-permute-start | bytes 3981320 | tf_op jit(solution)/shard_map/ppermute | solution.py:738
  82.3 4.5 %collective-permute-start.22 = (bf16[2,3,120,768]{3,2,1,0:T(8,128)(2,1)S(1)}, bf16[2,3,120,768]{3,2,1,0:T(8,128)(2,1)S(1)}, u32[]{:S(2)}, u32[]{:S(2)}) collective-permute-start(bf16[2,3,120,768]{3,2,1,0:T(8,128)(2,1)S(1)} %collective-permute-done.16.refs_3_), channel_id=1, source_target_pairs={{0,1},{1,0},{2,3},{3,2},{4,5},{5,4},{6,7},{7,6},{8,9},{9,8},{10,11... | collective-permute-start | bytes 3317768 | tf_op jit(solution)/shard_map/ppermute | solution.py:738
  82.9 3.2 %collective-permute-start.20 = (bf16[3,120,768]{2,1,0:T(8,128)(2,1)}, bf16[3,120,768]{2,1,0:T(8,128)(2,1)S(1)}, u32[]{:S(2)}, u32[]{:S(2)}) collective-permute-start(bf16[3,120,768]{2,1,0:T(8,128)(2,1)} %pad_maximum_fusion.10.refs_1_), channel_id=1, source_target_pairs={{0,1},{1,0},{2,3},{3,2},{4,5},{5,4},{6,7},{7,6},{8,9},{9,8},{10,11... | collective-permute-start | bytes 1658888 | tf_op jit(solution)/shard_map/ppermute | solution.py:738
  83.0 3.9 %collective-permute-start.21 = (bf16[3,120,768]{2,1,0:T(8,128)(2,1)}, bf16[3,120,768]{2,1,0:T(8,128)(2,1)S(1)}, u32[]{:S(2)}, u32[]{:S(2)}) collective-permute-start(bf16[3,120,768]{2,1,0:T(8,128)(2,1)} %collective-permute-done.7.refs_2_), channel_id=1, source_target_pairs={{0,1},{1,0},{2,3},{3,2},{4,5},{5,4},{6,7},{7,6},{8,9},{9,8},{10,11... | collective-permute-start | bytes 1658888 | tf_op jit(solution)/shard_map/ppermute | solution.py:738
  84.4 12.0 %collective-permute-start.18 = (bf16[3,96,768]{2,1,0:T(8,128)(2,1)S(1)}, bf16[3,96,768]{2,1,0:T(8,128)(2,1)S(1)}, u32[]{:S(2)}, u32[]{:S(2)}) collective-permute-start(bf16[3,96,768]{2,1,0:T(8,128)(2,1)S(1)} %pad_maximum_fusion.13.refs_3_), channel_id=1, source_target_pairs={{0,8},{1,17},{2,10},{3,19},{4,12},{5,21},{6,14},{7,23},{8,0},{9,25... | collective-permute-start | bytes 1327112 | tf_op jit(solution)/shard_map/ppermute | solution.py:743
  97.5 27.0 %collective-permute-start.23 = (bf16[2,3,96,768]{3,2,1,0:T(8,128)(2,1)}, bf16[2,3,96,768]{3,2,1,0:T(8,128)(2,1)}, u32[]{:S(2)}, u32[]{:S(2)}) collective-permute-start(bf16[2,3,96,768]{3,2,1,0:T(8,128)(2,1)} %pad_maximum_fusion.6), channel_id=1, source_target_pairs={{0,16},{1,9},{2,18},{3,11},{4,20},{5,13},{6,22},{7,15},{8,24},{9,1... | collective-permute-start | bytes 2654216 | tf_op jit(solution)/shard_map/ppermute | solution.py:743
  124.5 4.9 %collective-permute-start.24 = (bf16[4,4,96,768]{3,2,1,0:T(8,128)(2,1)}, bf16[4,4,96,768]{3,2,1,0:T(8,128)(2,1)S(1)}, u32[]{:S(2)}, u32[]{:S(2)}) collective-permute-start(bf16[4,4,96,768]{3,2,1,0:T(8,128)(2,1)} %get-tuple-element.139), channel_id=1, source_target_pairs={{0,1},{1,0},{2,3},{3,2},{4,5},{5,4},{6,7},{7,6},{8,9},{9,8},{10,11... | collective-permute-start | bytes 7077896 | tf_op jit(solution)/shard_map/ppermute | solution.py:738
  125.0 8.7 %collective-permute-start.27 = (bf16[2,3,96,768]{3,2,1,0:T(8,128)(2,1)}, bf16[2,3,96,768]{3,2,1,0:T(8,128)(2,1)}, u32[]{:S(2)}, u32[]{:S(2)}) collective-permute-start(bf16[2,3,96,768]{3,2,1,0:T(8,128)(2,1)} %collective-permute-done.23.refs_5_), channel_id=1, source_target_pairs={{0,1},{1,0},{2,3},{3,2},{4,5},{5,4},{6,7},{7,6},{8,9},{9,8},{10,11... | collective-permute-start | bytes 2654216 | tf_op jit(solution)/shard_map/ppermute | solution.py:738
  125.1 8.6 %collective-permute-start.25 = (bf16[3,96,768]{2,1,0:T(8,128)(2,1)S(1)}, bf16[3,96,768]{2,1,0:T(8,128)(2,1)S(1)}, u32[]{:S(2)}, u32[]{:S(2)}) collective-permute-start(bf16[3,96,768]{2,1,0:T(8,128)(2,1)S(1)} %copy-done.12), channel_id=1, source_target_pairs={{0,1},{1,0},{2,3},{3,2},{4,5},{5,4},{6,7},{7,6},{8,9},{9,8},{10,11... | collective-permute-start | bytes 1327112 | tf_op jit(solution)/shard_map/ppermute | solution.py:738
  125.6 8.2 %collective-permute-start.26 = (bf16[3,96,768]{2,1,0:T(8,128)(2,1)}, bf16[3,96,768]{2,1,0:T(8,128)(2,1)}, u32[]{:S(2)}, u32[]{:S(2)}) collective-permute-start(bf16[3,96,768]{2,1,0:T(8,128)(2,1)} %copy-done.22), channel_id=1, source_target_pairs={{0,1},{1,0},{2,3},{3,2},{4,5},{5,4},{6,7},{7,6},{8,9},{9,8},{10,11... | collective-permute-start | bytes 1327112 | tf_op jit(solution)/shard_map/ppermute | solution.py:738
  132.9 29.0 %collective-permute-start.28 = (bf16[2,4,96,768]{3,2,1,0:T(8,128)(2,1)}, bf16[2,4,96,768]{3,2,1,0:T(8,128)(2,1)}, u32[]{:S(2)}, u32[]{:S(2)}) collective-permute-start(bf16[2,4,96,768]{3,2,1,0:T(8,128)(2,1)} %pad_maximum_fusion.4), channel_id=1, source_target_pairs={{0,8},{1,17},{2,10},{3,19},{4,12},{5,21},{6,14},{7,23},{8,0},{9,25... | collective-permute-start | bytes 3538952 | tf_op jit(solution)/shard_map/ppermute | solution.py:743
  161.8 19.4 %collective-permute-start.30 = (bf16[4,4,96,768]{3,2,1,0:T(8,128)(2,1)}, bf16[4,4,96,768]{3,2,1,0:T(8,128)(2,1)}, u32[]{:S(2)}, u32[]{:S(2)}) collective-permute-start(bf16[4,4,96,768]{3,2,1,0:T(8,128)(2,1)} %get-tuple-element.151), channel_id=1, source_target_pairs={{0,1},{1,0},{2,3},{3,2},{4,5},{5,4},{6,7},{7,6},{8,9},{9,8},{10,11... | collective-permute-start | bytes 7077896 | tf_op jit(solution)/shard_map/ppermute | solution.py:738
  163.4 13.6 %collective-permute-start.29 = (bf16[4,96,768]{2,1,0:T(8,128)(2,1)S(1)}, bf16[4,96,768]{2,1,0:T(8,128)(2,1)}, u32[]{:S(2)}, u32[]{:S(2)}) collective-permute-start(bf16[4,96,768]{2,1,0:T(8,128)(2,1)S(1)} %fusion.15), channel_id=1, source_target_pairs={{0,16},{1,9},{2,18},{3,11},{4,20},{5,13},{6,22},{7,15},{8,24},{9,1... | collective-permute-start | bytes 1769480 | tf_op jit(solution)/shard_map/ppermute | solution.py:743
  176.8 3.5 %collective-permute-start.31 = (bf16[1,4,96,768]{3,2,1,0:T(8,128)(2,1)}, bf16[1,4,96,768]{3,2,1,0:T(8,128)(2,1)S(1)}, u32[]{:S(2)}, u32[]{:S(2)}) collective-permute-start(bf16[1,4,96,768]{3,2,1,0:T(8,128)(2,1)} %get-tuple-element.152), channel_id=1, source_target_pairs={{0,1},{1,0},{2,3},{3,2},{4,5},{5,4},{6,7},{7,6},{8,9},{9,8},{10,11... | collective-permute-start | bytes 1769480 | tf_op jit(solution)/shard_map/ppermute | solution.py:738
  179.5 28.2 %collective-permute-start.32 = (bf16[2,96,768]{2,1,0:T(8,128)(2,1)}, bf16[2,96,768]{2,1,0:T(8,128)(2,1)}, u32[]{:S(2)}, u32[]{:S(2)}) collective-permute-start(bf16[2,96,768]{2,1,0:T(8,128)(2,1)} %pad_maximum_fusion.19), channel_id=1, source_target_pairs={{0,2},{1,3},{2,0},{3,1},{4,6},{5,7},{6,4},{7,5},{8,10},{9,11},{10,... | collective-permute-start | bytes 884744 | tf_op jit(solution)/shard_map/ppermute | solution.py:738
  185.9 23.6 %collective-permute-start.33 = (bf16[2,4,120,768]{3,2,1,0:T(8,128)(2,1)}, bf16[2,4,120,768]{3,2,1,0:T(8,128)(2,1)}, u32[]{:S(2)}, u32[]{:S(2)}) collective-permute-start(bf16[2,4,120,768]{3,2,1,0:T(8,128)(2,1)} %pad_maximum_fusion.1), channel_id=1, source_target_pairs={{0,8},{1,17},{2,10},{3,19},{4,12},{5,21},{6,14},{7,23},{8,0},{9,25... | collective-permute-start | bytes 4423688 | tf_op jit(solution)/shard_map/ppermute | solution.py:743
  209.5 12.5 %collective-permute-start.35 = (bf16[96,768]{1,0:T(8,128)(2,1)}, bf16[96,768]{1,0:T(8,128)(2,1)}, u32[]{:S(2)}, u32[]{:S(2)}) collective-permute-start(bf16[96,768]{1,0:T(8,128)(2,1)} %get-tuple-element.202), channel_id=1, source_target_pairs={{0,4},{1,5},{2,6},{3,7},{4,0},{5,1},{6,2},{7,3},{8,12},{9,13},{10,... | collective-permute-start | bytes 442376 | tf_op jit(solution)/shard_map/ppermute | solution.py:738
  211.7 11.8 %collective-permute-start.34 = (bf16[4,120,768]{2,1,0:T(8,128)(2,1)}, bf16[4,120,768]{2,1,0:T(8,128)(2,1)}, u32[]{:S(2)}, u32[]{:S(2)}) collective-permute-start(bf16[4,120,768]{2,1,0:T(8,128)(2,1)} %fusion.7), channel_id=1, source_target_pairs={{0,16},{1,9},{2,18},{3,11},{4,20},{5,13},{6,22},{7,15},{8,24},{9,1... | collective-permute-start | bytes 2211848 | tf_op jit(solution)/shard_map/ppermute | solution.py:743
  223.5 4.5 %collective-permute-start.36 = (bf16[3,4,96,768]{3,2,1,0:T(8,128)(2,1)}, bf16[3,4,96,768]{3,2,1,0:T(8,128)(2,1)S(1)}, u32[]{:S(2)}, u32[]{:S(2)}) collective-permute-start(bf16[3,4,96,768]{3,2,1,0:T(8,128)(2,1)} %get-tuple-element.162), channel_id=1, source_target_pairs={{0,1},{1,0},{2,3},{3,2},{4,5},{5,4},{6,7},{7,6},{8,9},{9,8},{10,11... | collective-permute-start | bytes 5308424 | tf_op jit(solution)/shard_map/ppermute | solution.py:738
  226.8 13.7 %collective-permute-start.38 = (bf16[2,120,768]{2,1,0:T(8,128)(2,1)}, bf16[2,120,768]{2,1,0:T(8,128)(2,1)}, u32[]{:S(2)}, u32[]{:S(2)}) collective-permute-start(bf16[2,120,768]{2,1,0:T(8,128)(2,1)} %pad_maximum_fusion.15), channel_id=1, source_target_pairs={{0,2},{1,3},{2,0},{3,1},{4,6},{5,7},{6,4},{7,5},{8,10},{9,11},{10,... | collective-permute-start | bytes 1105928 | tf_op jit(solution)/shard_map/ppermute | solution.py:738
  229.5 13.4 %collective-permute-start.37 = (bf16[2,3,4,24,768]{4,3,2,1,0:T(8,128)(2,1)}, bf16[2,3,4,24,768]{4,3,2,1,0:T(8,128)(2,1)}, u32[]{:S(2)}, u32[]{:S(2)}) collective-permute-start(bf16[2,3,4,24,768]{4,3,2,1,0:T(8,128)(2,1)} %pad_maximum_fusion.7), channel_id=1, source_target_pairs={{0,8},{1,17},{2,10},{3,19},{4,12},{5,21},{6,14},{7,23},{8,0},{9,25... | collective-permute-start | bytes 2654216 | tf_op jit(solution)/shard_map/ppermute | solution.py:743
  244.9 8.6 %collective-permute-start.39 = (bf16[3,4,24,768]{3,2,1,0:T(8,128)(2,1)}, bf16[3,4,24,768]{3,2,1,0:T(8,128)(2,1)}, u32[]{:S(2)}, u32[]{:S(2)}) collective-permute-start(bf16[3,4,24,768]{3,2,1,0:T(8,128)(2,1)} %fusion.9), channel_id=1, source_target_pairs={{0,16},{1,9},{2,18},{3,11},{4,20},{5,13},{6,22},{7,15},{8,24},{9,1... | collective-permute-start | bytes 1327112 | tf_op jit(solution)/shard_map/ppermute | solution.py:743
  247.4 10.8 %collective-permute-start.44 = (bf16[120,768]{1,0:T(8,128)(2,1)S(1)}, bf16[120,768]{1,0:T(8,128)(2,1)S(1)}, u32[]{:S(2)}, u32[]{:S(2)}) collective-permute-start(bf16[120,768]{1,0:T(8,128)(2,1)S(1)} %fusion.25), channel_id=1, source_target_pairs={{0,4},{1,5},{2,6},{3,7},{4,0},{5,1},{6,2},{7,3},{8,12},{9,13},{10,... | collective-permute-start | bytes 552968 | tf_op jit(solution)/shard_map/ppermute | solution.py:738
  255.1 8.2 %collective-permute-start.42 = (bf16[2,80,768]{2,1,0:T(8,128)(2,1)S(1)}, bf16[2,80,768]{2,1,0:T(8,128)(2,1)S(1)}, u32[]{:S(2)}, u32[]{:S(2)}) collective-permute-start(bf16[2,80,768]{2,1,0:T(8,128)(2,1)S(1)} %pad_maximum_fusion.20), channel_id=1, source_target_pairs={{0,2},{1,3},{2,0},{3,1},{4,6},{5,7},{6,4},{7,5},{8,10},{9,11},{10,... | collective-permute-start | bytes 737288 | tf_op jit(solution)/shard_map/ppermute | solution.py:738
  259.2 7.2 %collective-permute-start.45 = (bf16[216,768]{1,0:T(8,128)(2,1)S(1)}, bf16[216,768]{1,0:T(8,128)(2,1)S(1)}, u32[]{:S(2)}, u32[]{:S(2)}) collective-permute-start(bf16[216,768]{1,0:T(8,128)(2,1)S(1)} %pad_maximum_fusion.17), channel_id=1, source_target_pairs={{0,8},{1,17},{2,10},{3,19},{4,12},{5,21},{6,14},{7,23},{8,0},{9,25... | collective-permute-start | bytes 995336 | tf_op jit(solution)/shard_map/ppermute | solution.py:743
  266.4 10.7 %collective-permute-start.46 = (bf16[2,216,768]{2,1,0:T(8,128)(2,1)S(1)}, bf16[2,216,768]{2,1,0:T(8,128)(2,1)S(1)}, u32[]{:S(2)}, u32[]{:S(2)}) collective-permute-start(bf16[2,216,768]{2,1,0:T(8,128)(2,1)S(1)} %pad_maximum_fusion.9), channel_id=1, source_target_pairs={{0,16},{1,9},{2,18},{3,11},{4,20},{5,13},{6,22},{7,15},{8,24},{9,1... | collective-permute-start | bytes 1990664 | tf_op jit(solution)/shard_map/ppermute | solution.py:743
  267.2 7.1 %collective-permute-start.43 = (bf16[80,768]{1,0:T(8,128)(2,1)S(1)}, bf16[80,768]{1,0:T(8,128)(2,1)S(1)}, u32[]{:S(2)}, u32[]{:S(2)}) collective-permute-start(bf16[80,768]{1,0:T(8,128)(2,1)S(1)} %fusion.33), channel_id=1, source_target_pairs={{0,4},{1,5},{2,6},{3,7},{4,0},{5,1},{6,2},{7,3},{8,12},{9,13},{10,... | collective-permute-start | bytes 368648 | tf_op jit(solution)/shard_map/ppermute | solution.py:738
  277.2 8.7 %collective-permute-start.47 = (bf16[80,768]{1,0:T(8,128)(2,1)S(1)}, bf16[80,768]{1,0:T(8,128)(2,1)S(1)}, u32[]{:S(2)}, u32[]{:S(2)}) collective-permute-start(bf16[80,768]{1,0:T(8,128)(2,1)S(1)} %fusion.23), channel_id=1, source_target_pairs={{0,8},{1,9},{2,10},{3,11},{4,12},{5,13},{6,14},{7,15},{8,0},{9,1},... | collective-permute-start | bytes 368648 | tf_op jit(solution)/shard_map/ppermute | solution.py:738
  277.8 8.1 %collective-permute-start.48 = (bf16[80,768]{1,0:T(8,128)(2,1)S(1)}, bf16[80,768]{1,0:T(8,128)(2,1)S(1)}, u32[]{:S(2)}, u32[]{:S(2)}) collective-permute-start(bf16[80,768]{1,0:T(8,128)(2,1)S(1)} %fusion.23), channel_id=1, source_target_pairs={{0,16},{1,17},{2,18},{3,19},{4,20},{5,21},{6,22},{7,23},{8,24},{9,... | collective-permute-start | bytes 368648 | tf_op jit(solution)/shard_map/ppermute | solution.py:738
  279.3 6.6 %collective-permute-start.49 = (bf16[80,768]{1,0:T(8,128)(2,1)S(1)}, bf16[80,768]{1,0:T(8,128)(2,1)S(1)}, u32[]{:S(2)}, u32[]{:S(2)}) collective-permute-start(bf16[80,768]{1,0:T(8,128)(2,1)S(1)} %fusion.23), channel_id=1, source_target_pairs={{0,24},{1,25},{2,26},{3,27},{4,28},{5,29},{6,30},{7,31},{8,16},{9,... | collective-permute-start | bytes 368648 | tf_op jit(solution)/shard_map/ppermute | solution.py:738
  (46 other events, 357.2 us)
